TPU v7x, 128 devices: a whole 4x4x4 slice. The times are simulated.
128 devices in a mesh: tm: 8 (over y_hi, z), rows: 16 (over y_lo, x, core).
Axes of the slice: x: 4, y: 4 (y_hi: 2, y_lo: 2; y = y_hi * 2 + y_lo), z: 4, core: 2. Of those that a mesh axis runs over, the one named last changes fastest.
Arguments:
- video: bfloat16 [1, 32, 128, 128, 256], P(None, 'tm', 'rows'), may hold values from -6 to 6
- spatial_weight: bfloat16 [2304, 256], P(('tm', 'rows')), may hold values from -0.125 to 0.125
- temporal_weight: bfloat16 [768, 256], P(('tm', 'rows')), may hold values from -0.21875 to 0.21875
- cotangent: bfloat16 [1, 32, 128, 128, 256], P(None, 'tm', 'rows'), may hold values from -6 to 6
Outputs:
- output: bfloat16 [1, 32, 128, 128, 256], P(None, 'tm', 'rows')
- grad_video: bfloat16 [1, 32, 128, 128, 256], P(None, 'tm', 'rows')
- grad_spatial: float32 [2304, 256], P(('tm', 'rows'))
- grad_temporal: float32 [768, 256], P(('tm', 'rows'))
All inputs are finite; a program needn't handle non-finite values.
Results may differ from a plain program's by a relative error of at most 0.0053.
Values may be sent and summed in bfloat16 or wider, within the bound.
No kernel may reach another device: no remote copies, remote signals or barrier semaphores. Data moves between devices by JAX's collectives and lax.ppermute only.
A program may use at most 128 MiB of HBM per device.

v0:
```python
import jax
import jax.numpy as jnp
import numpy as np
from jax import lax
from jax.experimental import pallas as pl
from jax.experimental.pallas import tpu as pltpu
from jax.sharding import PartitionSpec as P


epsilon = 1e-06
F32, BF16 = jnp.float32, jnp.bfloat16
AXES = ("tm", "rows")


def place(d):
    return d // 64, (d // 16) % 4, (d // 8) % 2, (d // 2) % 4, d % 2


def number(yh, z, yl, x, c):
    return ((yh * 4 + z) * 2 + yl) * 8 + x * 2 + c


def ring(axis):
    pairs = []
    for d in range(128):
        yh, z, yl, x, c = place(d)
        by = 1 - 2 * c
        if axis == "core":
            c = 1 - c
        elif axis == "x":
            x = (x + by) % 4
        elif axis == "z":
            z = (z + by) % 4
        else:
            y = (yh * 2 + yl + by) % 4
            yh, yl = y // 2, y % 2
        pairs.append((d, number(yh, z, yl, x, c)))
    return pairs


def moved(value, axis):
    return lax.ppermute(value, AXES, ring(axis))


def put(buf, part, *index):
    index = tuple(index) + (0,) * (buf.ndim - len(index))
    return lax.dynamic_update_slice(buf, part.reshape((1,) * (buf.ndim - part.ndim) + part.shape), index)


def take(value, index):
    return lax.dynamic_index_in_dim(value, index, 0, keepdims=False)


def gathered_axis(value, axis, mine, core):
    way = 1 - 2 * core
    full = moved(value, axis)
    half = moved(take(full, core), axis)
    other_full = moved(full, "core")
    other_half = moved(half, "core")
    buf = jnp.zeros((4,) + value.shape, value.dtype)
    buf = put(buf, value, mine)
    buf = put(buf, full, (mine - way) % 4)
    buf = put(buf, other_full, (mine + way) % 4)
    buf = put(buf, half, (mine + 2) % 4, core)
    return put(buf, other_half, (mine + 2) % 4, 1 - core)


def scattered_ring(own, send_half, keep_half, send_full, keep_full, axis, core):
    half = keep_half + moved(send_half, "core")
    full = keep_full + moved(send_full, "core")
    passed = moved(half, axis)
    full = put(full, take(full, core) + passed, core)
    return own + moved(full, axis)


def ring_blocks(value, mine, core):
    way = 1 - 2 * core
    opposite = take(value, (mine + 2) % 4)
    return (
        take(value, mine),
        take(opposite, 1 - core),
        take(opposite, core),
        take(value, (mine - way) % 4),
        take(value, (mine + way) % 4),
    )


def both_kernels(spatial, temporal, at):
    y, z, x, c = at
    chans = spatial.shape[1]
    rows_s, rows_t = spatial.shape[0], temporal.shape[0]
    own = jnp.concatenate([spatial, temporal], axis=0)
    other = moved(own, "core")
    pair = put(put(jnp.zeros((2,) + own.shape, own.dtype), own, c), other, 1 - c)
    rows = rows_s + rows_t
    units = gathered_axis(pair, "z", z, c)
    units = gathered_axis(units.reshape(2, 4 * rows, chans), "y", y, c)
    units = gathered_axis(units.reshape(2, 16 * rows, chans), "x", x, c)
    return units.reshape(4, 4, 4, 2 * rows, chans)


def unit_order(rows_s, rows_t):
    rows = rows_s + rows_t
    source = [rows * block + row for block in range(8) for row in range(rows_s)]
    source += [rows * block + rows_s + row for block in range(8) for row in range(rows_t)]
    return np.eye(8 * rows, dtype=np.float32)[source]


def summed_kernels(blocks, rows_s, rows_t, at):
    _, z, x, c = at
    chans = blocks[0].shape[-1]
    rows = 8 * (rows_s + rows_t)
    total = scattered_ring(*blocks, "y", c)
    total = total.reshape(4, 2, rows // 2, chans)
    total = scattered_ring(*ring_blocks(total, z, c), "z", c).reshape(rows, chans)
    total = jnp.concatenate(
        [
            total[: 8 * rows_s].reshape(4, 2, rows_s, chans),
            total[8 * rows_s :].reshape(4, 2, rows_t, chans),
        ],
        axis=2,
    )
    total = scattered_ring(*ring_blocks(total, x, c), "x", c)
    mine = take(total, c) + moved(take(total, 1 - c), "core")
    return mine[:rows_s], mine[rows_s:]


def traded_edges(inner, outer):
    count = lax.axis_size("rows")
    pairs = [(r, r + (1 if r % 2 else -1)) for r in range(count)]
    pairs = [(r, s) for r, s in pairs if 0 <= s < count]
    outer = lax.ppermute(outer, "rows", pairs)
    return moved(inner, "core"), outer


def edge_rows(value, core):
    last = value.shape[1] - 1
    inner = lax.dynamic_slice_in_dim(value, last * (1 - core), 1, 1)
    outer = lax.dynamic_slice_in_dim(value, last * core, 1, 1)
    return traded_edges(inner, outer)


def along_frames(value, by):
    count = lax.axis_size("tm")
    pairs = [(i, i + by) for i in range(count) if 0 <= i + by < count]
    return lax.ppermute(value, "tm", pairs)


def sigmoid(value):
    return 1.0 / (1.0 + jnp.exp(-value))


def dot(left, right):
    return jnp.dot(left, right, preferred_element_type=F32)


def contract(left, right):
    return lax.dot_general(left, right, (((0,), (0,)), ((), ())), preferred_element_type=F32)


def normalize(cells):
    inv_rms = lax.rsqrt(jnp.mean(cells * cells, axis=-1, keepdims=True) + epsilon)
    return cells * inv_rms, inv_rms


def store_shifts(out, row, value):
    cols, chans = value.shape
    col = lax.broadcasted_iota(jnp.int32, value.shape, 0)
    before = jnp.where(col == 0, 0.0, pltpu.roll(value, 1, 0))
    after = jnp.where(col == cols - 1, 0.0, pltpu.roll(value, cols - 1, 0))
    out[row, :, :chans] = before.astype(BF16)
    out[row, :, chans : 2 * chans] = value.astype(BF16)
    out[row, :, 2 * chans :] = after.astype(BF16)


def halo_row(row, n_rows, core, inner, outer, body):
    if row == 0:
        return jnp.where(core == 0, outer[0, 0], inner[0, 0])
    if row > n_rows:
        return jnp.where(core == 0, inner[0, 0], outer[0, 0])
    return body[0, row - 1]


def activate_kernel(at, video, inner, outer, _, shifts):
    n_rows = video.shape[1]
    for row in range(n_rows + 2):
        cells = halo_row(row, n_rows, at[1], inner, outer, video)
        normed, _ = normalize(cells.astype(F32))
        store_shifts(shifts.at[0], row, normed * sigmoid(normed))


def unit_number(y, z):
    return ((y // 2) * 4 + z) * 2 + y % 2


def assemble_kernel(order, units, w_s, w_t, w_back):
    chans = w_s.shape[1]
    rows_s, rows_t = w_s.shape[0] // 16, w_t.shape[0] // 16
    for y in range(4):
        for z in range(4):
            u = unit_number(y, z)
            blocks = jnp.concatenate([units[x, y, z] for x in range(4)], axis=0)
            unit = dot(order[...], blocks).astype(BF16)
            w_s[rows_s * u : rows_s * (u + 1)] = unit[:rows_s]
            w_t[rows_t * u : rows_t * (u + 1)] = unit[rows_s:]
    for k in range(3):
        w_back[chans * k : chans * (k + 1)] = w_t[chans * (2 - k) : chans * (3 - k)].T


def reverse_kernel(w_s, w_rev):
    chans = w_s.shape[1]
    for k in range(9):
        w_rev[chans * k : chans * (k + 1)] = w_s[chans * (8 - k) : chans * (9 - k)].T


def cot_window(frame, cot0, cot1, cot2, ahead1, ahead2, rows, last):
    return (
        cot0[0, rows],
        jnp.where(frame >= last, ahead1[0, rows], cot1[0, rows]),
        jnp.where(frame >= last - 1, ahead2[0, rows], cot2[0, rows]),
    )


def forward_kernel(
    at, shifts, cot0, cot1, cot2, ahead1, ahead2, w_s, w_back, hidden, grad_pre, inner, outer
):
    _, n_rows, n_cols, chans = hidden.shape
    step, frame = 4, at[2] + pl.program_id(0)
    for row in range(0, n_rows, step):
        pre = None
        for tap in range(3):
            left = shifts[0, row + tap : row + tap + step].reshape(step * n_cols, 3 * chans)
            term = dot(left, w_s[3 * chans * tap : 3 * chans * (tap + 1)])
            pre = term if pre is None else pre + term
        back = None
        window = cot_window(
            frame, cot0, cot1, cot2, ahead1, ahead2, slice(row, row + step), at[3]
        )
        for k, cot in enumerate(window):
            left = cot.reshape(step * n_cols, chans)
            term = dot(left, w_back[chans * k : chans * (k + 1)])
            back = term if back is None else back + term
        gate = sigmoid(pre)
        hidden[0, row : row + step] = (pre * gate).astype(BF16).reshape(step, n_cols, chans)
        slope = gate * (1.0 + pre * (1.0 - gate))
        grad_pre[0, row : row + step] = (back * slope).astype(BF16).reshape(step, n_cols, chans)
    first, final = grad_pre[0, 0], grad_pre[0, n_rows - 1]
    inner[0, 0] = jnp.where(at[1] == 0, final, first)
    outer[0, 0] = jnp.where(at[1] == 0, first, final)


def weights_kernel(
    at, shifts, grad_pre, hidden, cot0, cot1, cot2, ahead1, ahead2,
    own, send_half, keep_half, send_full, keep_full, grad_s, grad_t,
):
    @pl.when(pl.program_id(0) == 0)
    def _():
        grad_s[...] = jnp.zeros_like(grad_s)
        grad_t[...] = jnp.zeros_like(grad_t)

    _, n_rows, n_cols, chans = hidden.shape
    cells = n_rows * n_cols
    last = pl.num_programs(0) - 1
    frame = pl.program_id(0)
    right = grad_pre[0].reshape(cells, chans)
    for tap in range(3):
        left = shifts[0, tap : tap + n_rows].reshape(cells, 3 * chans)
        grad_s[3 * chans * tap : 3 * chans * (tap + 1)] += contract(left, right)
    left = hidden[0].reshape(cells, chans)
    window = cot_window(frame, cot0, cot1, cot2, ahead1, ahead2, slice(0, n_rows), last)
    for k, cot in enumerate(window[::-1]):
        grad_t[chans * k : chans * (k + 1)] += contract(left, cot.reshape(cells, chans))

    @pl.when(pl.program_id(0) == last)
    def _():
        rows_s, rows_t = 9 * chans // 16, 3 * chans // 16
        mine, core = at[0], at[1]
        way = 1 - 2 * core

        def fill(out, index, y, z):
            u = unit_number(y, z)
            top = (index % 2) * (rows_s + rows_t)
            at_s = pl.ds(pl.multiple_of(rows_s * u, rows_t), rows_s)
            at_t = pl.ds(pl.multiple_of(rows_t * u, rows_t), rows_t)
            target = out if out.ndim == 2 else out.at[index // 2]
            target[top : top + rows_s] = grad_s[at_s]
            target[top + rows_s : top + rows_s + rows_t] = grad_t[at_t]

        for z in range(4):
            fill(own, z, mine, z)
            fill(send_full, z, lax.rem(mine + 4 - way, 4), z)
            fill(keep_full, z, lax.rem(mine + 4 + way, 4), z)
        opposite = lax.rem(mine + 2, 4)
        for z in range(2):
            fill(send_half, z, opposite, 2 * (1 - core) + z)
            fill(keep_half, z, opposite, 2 * core + z)


def backward_kernel(at, grad_pre, inner, outer, video, cot, w_rev, _, grad_video, shifts):
    _, n_rows, n_cols, chans = video.shape
    for row in range(n_rows + 2):
        cells = halo_row(row, n_rows, at[1], inner, outer, grad_pre)
        store_shifts(shifts, row, cells.astype(F32))
    step = 4
    for row in range(0, n_rows, step):
        grad_act = None
        for tap in range(3):
            left = shifts[row + tap : row + tap + step].reshape(step * n_cols, 3 * chans)
            term = dot(left, w_rev[3 * chans * tap : 3 * chans * (tap + 1)])
            grad_act = term if grad_act is None else grad_act + term
        cells = video[0, row : row + step].reshape(step * n_cols, chans).astype(F32)
        normed, inv_rms = normalize(cells)
        gate = sigmoid(normed)
        grad_norm = grad_act * (gate * (1.0 + normed * (1.0 - gate)))
        along = jnp.mean(grad_norm * normed, axis=-1, keepdims=True)
        grad_in = inv_rms * (grad_norm - normed * along)
        total = cot[0, row : row + step].reshape(step * n_cols, chans).astype(F32) + grad_in
        grad_video[0, row : row + step] = total.astype(BF16).reshape(step, n_cols, chans)


def output_kernel(at, video, past0, past1, hid0, hid1, hid2, w_t, _, output):
    frame = pl.program_id(0)
    _, n_rows, n_cols, chans = video.shape
    step = 4
    for row in range(0, n_rows, step):
        rows = slice(row, row + step)
        parts = (
            jnp.where(frame < 2, past0[0, rows], hid0[0, rows]),
            jnp.where(frame < 1, past1[0, rows], hid1[0, rows]),
            hid2[0, rows],
        )
        left = jnp.concatenate([part.reshape(step * n_cols, chans) for part in parts], axis=-1)
        cells = video[0, rows].reshape(step * n_cols, chans).astype(F32)
        mixed = dot(left, w_t[...])
        output[0, rows] = (cells + mixed).astype(BF16).reshape(step, n_cols, chans)


def frame_spec(shape, index=lambda f: f):
    return pl.BlockSpec((1,) + tuple(shape[1:]), lambda f, *_: (index(f), 0, 0, 0))


def whole(shape):
    return pl.BlockSpec(
        tuple(shape), lambda f, *_: (0,) * len(shape), pipeline_mode=pl.Buffered(1)
    )


def call(
    body, n_frames, in_specs, out_specs, out_shape, flops, scratch=(), scalars=0, aliases={},
    limit=20,
):
    return pl.pallas_call(
        body,
        grid_spec=pltpu.PrefetchScalarGridSpec(
            num_scalar_prefetch=scalars,
            grid=(n_frames,),
            in_specs=in_specs,
            out_specs=out_specs,
            scratch_shapes=scratch,
        ),
        out_shape=out_shape,
        input_output_aliases=aliases,
        cost_estimate=pl.CostEstimate(flops=flops, bytes_accessed=8 << 20, transcendentals=0),
        compiler_params=pltpu.CompilerParams(vmem_limit_bytes=limit << 20),
    )


def part_of(body, part, parts, specs, out, args, flops, scratch=(), before=None):
    count = out.shape[0] // parts
    base = part * count
    in_specs = []
    for shape, index in specs:
        if index is None:
            in_specs.append(whole(shape))
        else:
            in_specs.append(frame_spec(shape, lambda f, g=index: g(f, base)))
    if before is None:
        in_specs.append(pl.BlockSpec(memory_space=pltpu.SMEM))
        before, aliases = jnp.zeros((1,), jnp.int32), {}
    else:
        in_specs.append(pl.BlockSpec(memory_space=pl.ANY))
        aliases = {len(args): 0}
    return call(
        body,
        count,
        in_specs,
        frame_spec(out.shape, lambda f: f + base),
        out,
        flops // parts,
        scratch,
        1,
        aliases,
    )(*args, before)


def single(body, out_shapes, flops, *args, limit=12):
    return pl.pallas_call(
        body,
        in_specs=[pl.BlockSpec(memory_space=pltpu.VMEM)] * len(args),
        out_specs=[pl.BlockSpec(memory_space=pltpu.VMEM)] * len(out_shapes),
        out_shape=[jax.ShapeDtypeStruct(shape, BF16) for shape in out_shapes],
        cost_estimate=pl.CostEstimate(flops=flops, bytes_accessed=3 << 20, transcendentals=0),
        compiler_params=pltpu.CompilerParams(vmem_limit_bytes=limit << 20),
    )(*args)


def residual_block(video, spatial_weight, temporal_weight, cotangent):
    _, n_frames, n_rows, n_cols, chans = video.shape
    t, r = lax.axis_index("tm"), lax.axis_index("rows")
    y, z, x, core = at = ((t // 4) * 2 + r // 8, t % 4, (r // 2) % 4, r % 2)
    video, cot = video[0], cotangent[0]
    shape = (n_frames, n_rows, n_cols, chans)
    wide = (n_frames, n_rows + 2, n_cols, 3 * chans)
    edge = (n_frames, 1, n_cols, chans)
    count = n_frames // 2
    half = (count,) + shape[1:]
    pair = 2 * n_frames * n_rows * n_cols * chans * chans
    rows_s, rows_t = spatial_weight.shape[0], temporal_weight.shape[0]
    rows = 8 * (rows_s + rows_t)
    last = n_frames - 1
    at_part = [jnp.stack([y, core, base, last]).astype(jnp.int32) for base in (0, count)]
    same = lambda f, base: f + base

    ahead = along_frames(cot[:2], -1)
    inner, outer = edge_rows(video, core)
    units = both_kernels(spatial_weight, temporal_weight, at)
    shifts = None
    for part in range(2):
        shifts = part_of(
            activate_kernel,
            part,
            2,
            [(shape, same), (edge, same), (edge, same)],
            jax.ShapeDtypeStruct(wide, BF16),
            (at_part[part], video, inner, outer),
            pair,
            before=shifts,
        )
    full_s, full_t = (9 * chans, chans), (3 * chans, chans)
    order = jnp.asarray(unit_order(rows_s, rows_t), BF16)
    w_s, w_t, w_back = single(assemble_kernel, (full_s, full_t, full_t), pair // 4, order, units)
    (w_rev,) = single(reverse_kernel, (full_s,), pair // 4, w_s)

    def cot_specs(base):
        specs = [
            frame_spec(shape, lambda f, k=k: jnp.minimum(f + base + k, last)) for k in range(3)
        ]
        return specs + [
            frame_spec(half, lambda f, k=k: jnp.maximum(f + base + k - last - 1, 0)) for k in (1, 2)
        ]

    hidden, grad_pre, edge_in, edge_out = call(
        forward_kernel,
        n_frames,
        [frame_spec(wide)] + cot_specs(0) + [whole(full_s), whole(full_t)],
        [frame_spec(shape)] * 2 + [frame_spec(edge)] * 2,
        [jax.ShapeDtypeStruct(shape, BF16)] * 2 + [jax.ShapeDtypeStruct(edge, BF16)] * 2,
        12 * pair,
        scalars=1,
    )(at_part[0], shifts, cot, cot, cot, ahead, ahead, w_s, w_back)
    edges = traded_edges(edge_in, edge_out)
    past = along_frames(hidden[count:], 1)
    block, half_block = (2, 2 * rows, chans), (2 * rows, chans)
    block_shapes = (block, half_block, half_block, block, block)
    blocks = call(
        weights_kernel,
        n_frames,
        [frame_spec(wide), frame_spec(shape), frame_spec(shape)] + cot_specs(0),
        [whole(shape_) for shape_ in block_shapes],
        [jax.ShapeDtypeStruct(shape_, F32) for shape_ in block_shapes],
        12 * pair,
        [pltpu.VMEM(full_s, F32), pltpu.VMEM(full_t, F32)],
        scalars=1,
        limit=28,
    )(at_part[0], shifts, grad_pre, hidden, cot, cot, cot, ahead, ahead)
    grad_video = part_of(
        backward_kernel,
        0,
        1,
        [(shape, same), (edge, same), (edge, same), (shape, same), (shape, same), (full_s, None)],
        jax.ShapeDtypeStruct(shape, BF16),
        (at_part[0], grad_pre, *edges, video, cot, w_rev),
        9 * pair,
        [pltpu.VMEM(wide[1:], BF16)],
    )
    output = part_of(
        output_kernel,
        0,
        1,
        [
            (shape, same),
            (half, lambda f, base: jnp.minimum(f, count - 1)),
            (half, lambda f, base: count - 1),
            (shape, lambda f, base: jnp.maximum(f - 2, 0)),
            (shape, lambda f, base: jnp.maximum(f - 1, 0)),
            (shape, same),
            (full_t, None),
        ],
        jax.ShapeDtypeStruct(shape, BF16),
        (at_part[0], video, past, past, hidden, hidden, hidden, w_t),
        3 * pair,
    )
    spatial_part, temporal_part = summed_kernels(blocks, rows_s, rows_t, at)
    total_cells = n_frames * n_rows * n_cols * lax.axis_size("tm") * lax.axis_size("rows")
    factor = float(total_cells) ** (-0.5)
    return (output[None], grad_video[None], spatial_part * factor, temporal_part * factor)


def solution(mesh):
    cells = P(None, "tm", "rows", None, None)
    kernels = P(("tm", "rows"), None)
    return jax.shard_map(
        residual_block,
        mesh=mesh,
        in_specs=(cells, kernels, kernels, cells),
        out_specs=(cells, cells, kernels, kernels),
        check_vma=False,
    )
```

profile of v0, /device:TPU:47, one launch (start us, length us, event | category | flops | bytes accessed | tf_op | source)
XLA Modules:
  0.0 162.3 jit_solution(11886160674101676746)
XLA Ops:
  4.4 2.8 %collective-permute-done.4 = bf16[2,24,256]{2,1,0:T(8,128)(2,1)S(1)} collective-permute-done((bf16[2,24,256]{2,1,0:T(8,128)(2,1)S(1)}, bf16[2,24,256]{2,1,0:T(8,128)(2,1)S(1)}, u32[]{:S(2)}, u32[]{:S(2)}) %collective-permute-start.4) | collective-permute-done | bytes 24608 | tf_op jit(solution)/shard_map/ppermute | solution.py:42
  7.2 1.7 %collective-permute-start.6 = (bf16[24,256]{1,0:T(8,128)(2,1)S(1)}, bf16[24,256]{1,0:T(8,128)(2,1)S(1)}, u32[]{:S(2)}, u32[]{:S(2)}) collective-permute-start(bf16[24,256]{1,0:T(8,128)(2,1)S(1)} %dynamic-slice_bitcast_fusion.7), channel_id=1, source_target_pairs={{0,16},{1,49},{2,18},{3,51},{4,20},{5,53},{6,22},{7,55},{8,24},{9,... | collective-permute-start | bytes 36872 | tf_op jit(solution)/shard_map/ppermute | solution.py:42
  8.9 3.4 %collective-permute-start.5 = (bf16[2,24,256]{2,1,0:T(8,128)(2,1)S(1)}, bf16[2,24,256]{2,1,0:T(8,128)(2,1)S(1)}, u32[]{:S(2)}, u32[]{:S(2)}) collective-permute-start(bf16[2,24,256]{2,1,0:T(8,128)(2,1)S(1)} %collective-permute-done.4), channel_id=1, source_target_pairs={{0,1},{1,0},{2,3},{3,2},{4,5},{5,4},{6,7},{7,6},{8,9},{9,8},{10,11... | collective-permute-start | bytes 73736 | tf_op jit(solution)/shard_map/ppermute | solution.py:42
  12.3 1.9 %collective-permute-start.7 = (bf16[24,256]{1,0:T(8,128)(2,1)S(1)}, bf16[24,256]{1,0:T(8,128)(2,1)S(1)}, u32[]{:S(2)}, u32[]{:S(2)}) collective-permute-start(bf16[24,256]{1,0:T(8,128)(2,1)S(1)} %collective-permute-done.6), channel_id=1, source_target_pairs={{0,1},{1,0},{2,3},{3,2},{4,5},{5,4},{6,7},{7,6},{8,9},{9,8},{10,11... | collective-permute-start | bytes 36872 | tf_op jit(solution)/shard_map/ppermute | solution.py:42
  15.2 3.5 %collective-permute-done.8 = bf16[2,96,256]{2,1,0:T(8,128)(2,1)S(1)} collective-permute-done((bf16[2,96,256]{2,1,0:T(8,128)(2,1)S(1)}, bf16[2,96,256]{2,1,0:T(8,128)(2,1)S(1)}, u32[]{:S(2)}, u32[]{:S(2)}) %collective-permute-start.8) | collective-permute-done | bytes 98336 | tf_op jit(solution)/shard_map/ppermute | solution.py:42
  19.5 2.0 %collective-permute-start.9 = (bf16[2,96,256]{2,1,0:T(8,128)(2,1)S(1)}, bf16[2,96,256]{2,1,0:T(8,128)(2,1)S(1)}, u32[]{:S(2)}, u32[]{:S(2)}) collective-permute-start(bf16[2,96,256]{2,1,0:T(8,128)(2,1)S(1)} %collective-permute-done.8), channel_id=1, source_target_pairs={{0,1},{1,0},{2,3},{3,2},{4,5},{5,4},{6,7},{7,6},{8,9},{9,8},{10,11... | collective-permute-start | bytes 294920 | tf_op jit(solution)/shard_map/ppermute | solution.py:42
  21.7 2.3 %collective-permute-start.11 = (bf16[96,256]{1,0:T(8,128)(2,1)S(1)}, bf16[96,256]{1,0:T(8,128)(2,1)S(1)}, u32[]{:S(2)}, u32[]{:S(2)}) collective-permute-start(bf16[96,256]{1,0:T(8,128)(2,1)S(1)} %collective-permute-done.10), channel_id=1, source_target_pairs={{0,1},{1,0},{2,3},{3,2},{4,5},{5,4},{6,7},{7,6},{8,9},{9,8},{10,11... | collective-permute-start | bytes 147464 | tf_op jit(solution)/shard_map/ppermute | solution.py:42
  26.2 5.0 %collective-permute-start.2 = (bf16[2,8,128,256]{3,2,1,0:T(8,128)(2,1)}, bf16[2,8,128,256]{3,2,1,0:T(8,128)(2,1)}, u32[]{:S(2)}, u32[]{:S(2)}) collective-permute-start(bf16[2,8,128,256]{3,2,1,0:T(8,128)(2,1)} %slice_bitcast_fusion), channel_id=1, source_target_pairs={{16,0},{32,16},{48,32},{64,48},{80,64},{96,80},{112,96},{17,1},{33... | collective-permute-start | bytes 3145736 | tf_op jit(solution)/shard_map/ppermute | solution.py:146
  34.3 2.2 %shard_map.84._ = bf16[4,10,128,768]{3,2,1,0:T(8,128)(2,1)S(1)} custom-call(s32[4]{0:T(128)S(1)} %get-tuple-element.33.at, bf16[4,8,128,256]{3,2,1,0:T(8,128)(2,1)S(1)} %bitcast.103, bf16[4,1,128,256]{3,2,1,0:T(8,128)(2,1)S(1)} %collective-permute-done.inner, bf16[4,1,128,256]{3,2,1,0:T(8,128)(2,1)S(1)} %collective-permute-done.1.outer, s32[1]{0:T(128)} %constant.271.clone.1._), custom_call_target="tpu_custom_call" | custom-call | flops 268435456 | bytes 8388608 | tf_op jit(solution)/shard_map/pallas_call | solution.py:383
  36.5 2.2 %shard_map.85.shifts = bf16[4,10,128,768]{3,2,1,0:T(8,128)(2,1)S(1)} custom-call(s32[4]{0:T(128)S(1)} %get-tuple-element.32.at, bf16[4,8,128,256]{3,2,1,0:T(8,128)(2,1)S(1)} %bitcast.104, bf16[4,1,128,256]{3,2,1,0:T(8,128)(2,1)S(1)} %collective-permute-done.inner, ...), custom_call_target="tpu_custom_call", output_to_operand_aliasing={{}: (4, {})} | custom-call | flops 268435456 | bytes 8388608 | tf_op jit(solution)/shard_map/pallas_call | solution.py:383
  40.8 4.7 %collective-permute-done.14 = bf16[384,256]{1,0:T(8,128)(2,1)S(1)} collective-permute-done((bf16[384,256]{1,0:T(8,128)(2,1)S(1)}, bf16[384,256]{1,0:T(8,128)(2,1)S(1)}, u32[]{:S(2)}, u32[]{:S(2)}) %collective-permute-start.14) | collective-permute-done | bytes 196640 | tf_op jit(solution)/shard_map/ppermute | solution.py:42
  48.4 3.2 %collective-permute-done.2.ahead1.ahead2 = bf16[2,8,128,256]{3,2,1,0:T(8,128)(2,1)} collective-permute-done((bf16[2,8,128,256]{3,2,1,0:T(8,128)(2,1)}, bf16[2,8,128,256]{3,2,1,0:T(8,128)(2,1)}, u32[]{:S(2)}, u32[]{:S(2)}) %collective-permute-start.2) | collective-permute-done | bytes 1048608 | tf_op jit(solution)/shard_map/ppermute | solution.py:146
  51.7 10.3 %shard_map.87 = (bf16[4,8,128,256]{3,2,1,0:T(8,128)(2,1)S(1)}, bf16[4,8,128,256]{3,2,1,0:T(8,128)(2,1)S(1)}, bf16[4,1,128,256]{3,2,1,0:T(8,128)(2,1)}, bf16[4,1,128,256]{3,2,1,0:T(8,128)(2,1)S(1)}) custom-call(s32[4]{0:T(128)S(1)} %get-tuple-element.33.at, bf16[4,10,128,768]{3,2,1,0:T(8,128)(2,1)S(1)} %shard_map.85.shifts, ...), custom_call_target="tpu_custom_call" | custom-call | flops 6442450944 | bytes 8388608 | tf_op jit(solution)/shard_map/pallas_call | solution.py:452
  62.0 10.1 %shard_map.91 = (f32[2,384,256]{2,1,0:T(8,128)S(1)}, f32[384,256]{1,0:T(8,128)S(1)}, f32[384,256]{1,0:T(8,128)S(1)}, f32[2,384,256]{2,1,0:T(8,128)S(1)}, f32[2,384,256]{2,1,0:T(8,128)S(1)}) custom-call(s32[4]{0:T(128)S(1)} %get-tuple-element.33.at, bf16[4,10,128,768]{3,2,1,0:T(8,128)(2,1)S(1)} %shard_map.85.shifts, ...), custom_call_target="tpu_custom_call" | custom-call | flops 6442450944 | bytes 8388608 | tf_op jit(solution)/shard_map/pallas_call | solution.py:465
  73.0 3.2 %collective-permute-start.19 = (f32[2,384,256]{2,1,0:T(8,128)S(1)}, f32[2,384,256]{2,1,0:T(8,128)S(1)}, u32[]{:S(2)}, u32[]{:S(2)}) collective-permute-start(f32[2,384,256]{2,1,0:T(8,128)S(1)} %get-tuple-element.25), channel_id=1, source_target_pairs={{0,1},{1,0},{2,3},{3,2},{4,5},{5,4},{6,7},{7,6},{8,9},{9,8},{10,11... | collective-permute-start | bytes 2359304 | tf_op jit(solution)/shard_map/ppermute | solution.py:42
  76.3 2.5 %collective-permute-done.20 = f32[384,256]{1,0:T(8,128)S(1)} collective-permute-done((f32[384,256]{1,0:T(8,128)S(1)}, f32[384,256]{1,0:T(8,128)S(1)}, u32[]{:S(2)}, u32[]{:S(2)}) %collective-permute-start.20) | collective-permute-done | bytes 393248 | tf_op jit(solution)/shard_map/ppermute | solution.py:42
  78.8 2.7 %collective-permute-start.21 = (f32[384,256]{1,0:T(8,128)S(1)}, f32[384,256]{1,0:T(8,128)S(1)}, u32[]{:S(2)}, u32[]{:S(2)}) collective-permute-start(f32[384,256]{1,0:T(8,128)S(1)} %add.257), channel_id=1, source_target_pairs={{0,8},{1,73},{2,10},{3,75},{4,12},{5,77},{6,14},{7,79},{8,64},{9,1... | collective-permute-start | bytes 1179656 | tf_op jit(solution)/shard_map/ppermute | solution.py:42
  83.5 2.7 %collective-permute-done.21 = f32[384,256]{1,0:T(8,128)S(1)} collective-permute-done((f32[384,256]{1,0:T(8,128)S(1)}, f32[384,256]{1,0:T(8,128)S(1)}, u32[]{:S(2)}, u32[]{:S(2)}) %collective-permute-start.21) | collective-permute-done | bytes 393248 | tf_op jit(solution)/shard_map/ppermute | solution.py:42
  87.0 2.2 %collective-permute-start.22 = (f32[2,384,256]{2,1,0:T(8,128)}, f32[2,384,256]{2,1,0:T(8,128)}, u32[]{:S(2)}, u32[]{:S(2)}) collective-permute-start(f32[2,384,256]{2,1,0:T(8,128)} %bitcast_dynamic-update-slice_fusion), channel_id=1, source_target_pairs={{0,8},{1,73},{2,10},{3,75},{4,12},{5,77},{6,14},{7,79},{8,64},{9,1... | collective-permute-start | bytes 2359304 | tf_op jit(solution)/shard_map/ppermute | solution.py:42
  89.2 9.3 %collective-permute-done.22 = f32[2,384,256]{2,1,0:T(8,128)} collective-permute-done((f32[2,384,256]{2,1,0:T(8,128)}, f32[2,384,256]{2,1,0:T(8,128)}, u32[]{:S(2)}, u32[]{:S(2)}) %collective-permute-start.22) | collective-permute-done | bytes 786464 | tf_op jit(solution)/shard_map/ppermute | solution.py:42
  100.0 3.8 %collective-permute-start.24 = (f32[96,256]{1,0:T(8,128)S(1)}, f32[96,256]{1,0:T(8,128)S(1)}, u32[]{:S(2)}, u32[]{:S(2)}) collective-permute-start(f32[96,256]{1,0:T(8,128)S(1)} %dynamic-slice_bitcast_fusion.4), channel_id=1, source_target_pairs={{0,1},{1,0},{2,3},{3,2},{4,5},{5,4},{6,7},{7,6},{8,9},{9,8},{10,11... | collective-permute-start | bytes 294920 | tf_op jit(solution)/shard_map/ppermute | solution.py:42
  104.8 2.3 %collective-permute-start.25 = (f32[96,256]{1,0:T(8,128)S(1)}, f32[96,256]{1,0:T(8,128)S(1)}, u32[]{:S(2)}, u32[]{:S(2)}) collective-permute-start(f32[96,256]{1,0:T(8,128)S(1)} %bitcast_add_fusion.3), channel_id=1, source_target_pairs={{0,16},{1,49},{2,18},{3,51},{4,20},{5,53},{6,22},{7,55},{8,24},{9,... | collective-permute-start | bytes 294920 | tf_op jit(solution)/shard_map/ppermute | solution.py:42
  109.3 5.1 %collective-permute-start.26 = (f32[2,96,256]{2,1,0:T(8,128)}, f32[2,96,256]{2,1,0:T(8,128)}, u32[]{:S(2)}, u32[]{:S(2)}) collective-permute-start(f32[2,96,256]{2,1,0:T(8,128)} %bitcast_dynamic-update-slice_fusion.5), channel_id=1, source_target_pairs={{0,16},{1,49},{2,18},{3,51},{4,20},{5,53},{6,22},{7,55},{8,24},{9,... | collective-permute-start | bytes 589832 | tf_op jit(solution)/shard_map/ppermute | solution.py:42
  119.1 4.0 %collective-permute-start.16 = (bf16[2,8,128,256]{3,2,1,0:T(8,128)(2,1)}, bf16[2,8,128,256]{3,2,1,0:T(8,128)(2,1)S(1)}, u32[]{:S(2)}, u32[]{:S(2)}) collective-permute-start(bf16[2,8,128,256]{3,2,1,0:T(8,128)(2,1)} %slice.23), channel_id=1, source_target_pairs={{0,16},{16,32},{32,48},{48,64},{64,80},{80,96},{96,112},{1,17},{17... | collective-permute-start | bytes 3145736 | tf_op jit(solution)/shard_map/ppermute | solution.py:146
  124.9 1.6 reshape.116
  127.2 1.8 %collective-permute-start.28 = (f32[24,256]{1,0:T(8,128)S(1)}, f32[24,256]{1,0:T(8,128)S(1)}, u32[]{:S(2)}, u32[]{:S(2)}) collective-permute-start(f32[24,256]{1,0:T(8,128)S(1)} %fusion.9), channel_id=1, source_target_pairs={{0,1},{1,0},{2,3},{3,2},{4,5},{5,4},{6,7},{7,6},{8,9},{9,8},{10,11... | collective-permute-start | bytes 73736 | tf_op jit(solution)/shard_map/ppermute | solution.py:42
  132.7 3.9 %collective-permute-done.29 = f32[24,256]{1,0:T(8,128)S(1)} collective-permute-done((f32[24,256]{1,0:T(8,128)S(1)}, f32[24,256]{1,0:T(8,128)S(1)}, u32[]{:S(2)}, u32[]{:S(2)}) %collective-permute-start.29) | collective-permute-done | bytes 24608 | tf_op jit(solution)/shard_map/ppermute | solution.py:42
  139.6 1.6 copy-done.7
  141.2 1.6 copy-done.12
  142.8 9.8 %shard_map.90 = bf16[4,8,128,256]{3,2,1,0:T(8,128)(2,1)} custom-call(s32[4]{0:T(128)S(1)} %get-tuple-element.33.at, bf16[4,8,128,256]{3,2,1,0:T(8,128)(2,1)S(1)} %copy-done.12, bf16[4,1,128,256]{3,2,1,0:T(8,128)(2,1)} %collective-permute-done.17.inner, bf16[4,1,128,256]{3,2,1,0:T(8,128)(2,1)} %collective-permute-done.18.outer, ...), custom_call_target="tpu_custom_call" | custom-call | flops 4831838208 | bytes 8388608 | tf_op jit(solution)/shard_map/pallas_call | solution.py:383
  152.6 4.6 %collective-permute-start.31 = (f32[24,256]{1,0:T(8,128)S(1)}, f32[24,256]{1,0:T(8,128)S(1)}, u32[]{:S(2)}, u32[]{:S(2)}) collective-permute-start(f32[24,256]{1,0:T(8,128)S(1)} %dynamic-slice_bitcast_fusion.6), channel_id=1, source_target_pairs={{0,1},{1,0},{2,3},{3,2},{4,5},{5,4},{6,7},{7,6},{8,9},{9,8},{10,11... | collective-permute-start | bytes 73736 | tf_op jit(solution)/shard_map/ppermute | solution.py:42
  157.2 3.9 %shard_map.88 = bf16[4,8,128,256]{3,2,1,0:T(8,128)(2,1)} custom-call(s32[4]{0:T(128)S(1)} %get-tuple-element.33.at, bf16[4,8,128,256]{3,2,1,0:T(8,128)(2,1)S(1)} %bitcast.106, bf16[2,8,128,256]{3,2,1,0:T(8,128)(2,1)S(1)} %collective-permute-done.16.past0.past1, bf16[2,8,128,256]{3,2,1,0:T(8,128)(2,1)S(1)} %collective-permute-done.16.past0.past1, ...), custom_call_target="tpu_custom_call" | custom-call | flops 1610612736 | bytes 8388608 | tf_op jit(solution)/shard_map/pallas_call | solution.py:383
  (125 shorter events, 39.2 us)
Async XLA Ops:
  1.6 2.7 %collective-permute-start.3 = (bf16[24,256]{1,0:T(8,128)(2,1)S(1)}, bf16[24,256]{1,0:T(8,128)(2,1)S(1)}, u32[]{:S(2)}, u32[]{:S(2)}) collective-permute-start(bf16[24,256]{1,0:T(8,128)(2,1)S(1)} %get-tuple-element.29), channel_id=1, source_target_pairs={{0,1},{1,0},{2,3},{3,2},{4,5},{5,4},{6,7},{7,6},{8,9},{9,8},{10,11... | collective-permute-start | bytes 36872 | tf_op jit(solution)/shard_map/ppermute | solution.py:42
  3.3 31.0 %collective-permute-start = (bf16[4,1,128,256]{3,2,1,0:T(8,128)(2,1)S(1)}, bf16[4,1,128,256]{3,2,1,0:T(8,128)(2,1)S(1)}, u32[]{:S(2)}, u32[]{:S(2)}) collective-permute-start(bf16[4,1,128,256]{3,2,1,0:T(8,128)(2,1)S(1)} %get-tuple-element.31), channel_id=1, source_target_pairs={{0,1},{1,0},{2,3},{3,2},{4,5},{5,4},{6,7},{7,6},{8,9},{9,8},{10,11... | collective-permute-start | bytes 786440 | tf_op jit(solution)/shard_map/ppermute | solution.py:42
  3.4 30.9 %collective-permute-start.1 = (bf16[4,1,128,256]{3,2,1,0:T(8,128)(2,1)S(1)}, bf16[4,1,128,256]{3,2,1,0:T(8,128)(2,1)S(1)}, u32[]{:S(2)}, u32[]{:S(2)}) collective-permute-start(bf16[4,1,128,256]{3,2,1,0:T(8,128)(2,1)S(1)} %get-tuple-element.30), channel_id=1, source_target_pairs={{1,2},{2,1},{3,4},{4,3},{5,6},{6,5},{7,8},{8,7},{9,10},{10,9},{11,... | collective-permute-start | bytes 786440 | tf_op jit(solution)/shard_map/ppermute | solution.py:132
  4.3 2.9 %collective-permute-start.4 = (bf16[2,24,256]{2,1,0:T(8,128)(2,1)S(1)}, bf16[2,24,256]{2,1,0:T(8,128)(2,1)S(1)}, u32[]{:S(2)}, u32[]{:S(2)}) collective-permute-start(bf16[2,24,256]{2,1,0:T(8,128)(2,1)S(1)} %bitcast_dynamic-update-slice_fusion.16), channel_id=1, source_target_pairs={{0,16},{1,49},{2,18},{3,51},{4,20},{5,53},{6,22},{7,55},{8,24},{9,... | collective-permute-start | bytes 73736 | tf_op jit(solution)/shard_map/ppermute | solution.py:42
  7.2 5.1 %collective-permute-start.6 = (bf16[24,256]{1,0:T(8,128)(2,1)S(1)}, bf16[24,256]{1,0:T(8,128)(2,1)S(1)}, u32[]{:S(2)}, u32[]{:S(2)}) collective-permute-start(bf16[24,256]{1,0:T(8,128)(2,1)S(1)} %dynamic-slice_bitcast_fusion.7), channel_id=1, source_target_pairs={{0,16},{1,49},{2,18},{3,51},{4,20},{5,53},{6,22},{7,55},{8,24},{9,... | collective-permute-start | bytes 36872 | tf_op jit(solution)/shard_map/ppermute | solution.py:42
  8.9 5.3 %collective-permute-start.5 = (bf16[2,24,256]{2,1,0:T(8,128)(2,1)S(1)}, bf16[2,24,256]{2,1,0:T(8,128)(2,1)S(1)}, u32[]{:S(2)}, u32[]{:S(2)}) collective-permute-start(bf16[2,24,256]{2,1,0:T(8,128)(2,1)S(1)} %collective-permute-done.4), channel_id=1, source_target_pairs={{0,1},{1,0},{2,3},{3,2},{4,5},{5,4},{6,7},{7,6},{8,9},{9,8},{10,11... | collective-permute-start | bytes 73736 | tf_op jit(solution)/shard_map/ppermute | solution.py:42
  12.3 2.7 %collective-permute-start.7 = (bf16[24,256]{1,0:T(8,128)(2,1)S(1)}, bf16[24,256]{1,0:T(8,128)(2,1)S(1)}, u32[]{:S(2)}, u32[]{:S(2)}) collective-permute-start(bf16[24,256]{1,0:T(8,128)(2,1)S(1)} %collective-permute-done.6), channel_id=1, source_target_pairs={{0,1},{1,0},{2,3},{3,2},{4,5},{5,4},{6,7},{7,6},{8,9},{9,8},{10,11... | collective-permute-start | bytes 36872 | tf_op jit(solution)/shard_map/ppermute | solution.py:42
  15.0 3.8 %collective-permute-start.8 = (bf16[2,96,256]{2,1,0:T(8,128)(2,1)S(1)}, bf16[2,96,256]{2,1,0:T(8,128)(2,1)S(1)}, u32[]{:S(2)}, u32[]{:S(2)}) collective-permute-start(bf16[2,96,256]{2,1,0:T(8,128)(2,1)S(1)} %bitcast.125), channel_id=1, source_target_pairs={{0,8},{1,73},{2,10},{3,75},{4,12},{5,77},{6,14},{7,79},{8,64},{9,1... | collective-permute-start | bytes 294920 | tf_op jit(solution)/shard_map/ppermute | solution.py:42
  18.8 2.9 %collective-permute-start.10 = (bf16[96,256]{1,0:T(8,128)(2,1)S(1)}, bf16[96,256]{1,0:T(8,128)(2,1)S(1)}, u32[]{:S(2)}, u32[]{:S(2)}) collective-permute-start(bf16[96,256]{1,0:T(8,128)(2,1)S(1)} %dynamic-slice_bitcast_fusion.5), channel_id=1, source_target_pairs={{0,8},{1,73},{2,10},{3,75},{4,12},{5,77},{6,14},{7,79},{8,64},{9,1... | collective-permute-start | bytes 147464 | tf_op jit(solution)/shard_map/ppermute | solution.py:42
  19.5 4.5 %collective-permute-start.9 = (bf16[2,96,256]{2,1,0:T(8,128)(2,1)S(1)}, bf16[2,96,256]{2,1,0:T(8,128)(2,1)S(1)}, u32[]{:S(2)}, u32[]{:S(2)}) collective-permute-start(bf16[2,96,256]{2,1,0:T(8,128)(2,1)S(1)} %collective-permute-done.8), channel_id=1, source_target_pairs={{0,1},{1,0},{2,3},{3,2},{4,5},{5,4},{6,7},{7,6},{8,9},{9,8},{10,11... | collective-permute-start | bytes 294920 | tf_op jit(solution)/shard_map/ppermute | solution.py:42
  21.7 3.2 %collective-permute-start.11 = (bf16[96,256]{1,0:T(8,128)(2,1)S(1)}, bf16[96,256]{1,0:T(8,128)(2,1)S(1)}, u32[]{:S(2)}, u32[]{:S(2)}) collective-permute-start(bf16[96,256]{1,0:T(8,128)(2,1)S(1)} %collective-permute-done.10), channel_id=1, source_target_pairs={{0,1},{1,0},{2,3},{3,2},{4,5},{5,4},{6,7},{7,6},{8,9},{9,8},{10,11... | collective-permute-start | bytes 147464 | tf_op jit(solution)/shard_map/ppermute | solution.py:42
  24.9 7.9 %collective-permute-start.12 = (bf16[2,384,256]{2,1,0:T(8,128)(2,1)S(1)}, bf16[2,384,256]{2,1,0:T(8,128)(2,1)}, u32[]{:S(2)}, u32[]{:S(2)}) collective-permute-start(bf16[2,384,256]{2,1,0:T(8,128)(2,1)S(1)} %bitcast.121), channel_id=1, source_target_pairs={{0,2},{1,7},{2,4},{3,1},{4,6},{5,3},{6,0},{7,5},{8,10},{9,15},{10,... | collective-permute-start | bytes 1179656 | tf_op jit(solution)/shard_map/ppermute | solution.py:42
  26.2 25.4 %collective-permute-start.2 = (bf16[2,8,128,256]{3,2,1,0:T(8,128)(2,1)}, bf16[2,8,128,256]{3,2,1,0:T(8,128)(2,1)}, u32[]{:S(2)}, u32[]{:S(2)}) collective-permute-start(bf16[2,8,128,256]{3,2,1,0:T(8,128)(2,1)} %slice_bitcast_fusion), channel_id=1, source_target_pairs={{16,0},{32,16},{48,32},{64,48},{80,64},{96,80},{112,96},{17,1},{33... | collective-permute-start | bytes 3145736 | tf_op jit(solution)/shard_map/ppermute | solution.py:146
  32.9 12.6 %collective-permute-start.13 = (bf16[2,384,256]{2,1,0:T(8,128)(2,1)}, bf16[2,384,256]{2,1,0:T(8,128)(2,1)S(1)}, u32[]{:S(2)}, u32[]{:S(2)}) collective-permute-start(bf16[2,384,256]{2,1,0:T(8,128)(2,1)} %collective-permute-done.12), channel_id=1, source_target_pairs={{0,1},{1,0},{2,3},{3,2},{4,5},{5,4},{6,7},{7,6},{8,9},{9,8},{10,11... | collective-permute-start | bytes 1179656 | tf_op jit(solution)/shard_map/ppermute | solution.py:42
  39.7 5.8 %collective-permute-start.14 = (bf16[384,256]{1,0:T(8,128)(2,1)S(1)}, bf16[384,256]{1,0:T(8,128)(2,1)S(1)}, u32[]{:S(2)}, u32[]{:S(2)}) collective-permute-start(bf16[384,256]{1,0:T(8,128)(2,1)S(1)} %dynamic-slice_bitcast_fusion.3), channel_id=1, source_target_pairs={{0,2},{1,7},{2,4},{3,1},{4,6},{5,3},{6,0},{7,5},{8,10},{9,15},{10,... | collective-permute-start | bytes 589832 | tf_op jit(solution)/shard_map/ppermute | solution.py:42
  45.5 1.4 collective-permute-start.15
  73.0 8.4 %collective-permute-start.19 = (f32[2,384,256]{2,1,0:T(8,128)S(1)}, f32[2,384,256]{2,1,0:T(8,128)S(1)}, u32[]{:S(2)}, u32[]{:S(2)}) collective-permute-start(f32[2,384,256]{2,1,0:T(8,128)S(1)} %get-tuple-element.25), channel_id=1, source_target_pairs={{0,1},{1,0},{2,3},{3,2},{4,5},{5,4},{6,7},{7,6},{8,9},{9,8},{10,11... | collective-permute-start | bytes 2359304 | tf_op jit(solution)/shard_map/ppermute | solution.py:42
  76.3 2.5 %collective-permute-start.20 = (f32[384,256]{1,0:T(8,128)S(1)}, f32[384,256]{1,0:T(8,128)S(1)}, u32[]{:S(2)}, u32[]{:S(2)}) collective-permute-start(f32[384,256]{1,0:T(8,128)S(1)} %get-tuple-element.27), channel_id=1, source_target_pairs={{0,1},{1,0},{2,3},{3,2},{4,5},{5,4},{6,7},{7,6},{8,9},{9,8},{10,11... | collective-permute-start | bytes 1179656 | tf_op jit(solution)/shard_map/ppermute | solution.py:42
  78.8 7.4 %collective-permute-start.21 = (f32[384,256]{1,0:T(8,128)S(1)}, f32[384,256]{1,0:T(8,128)S(1)}, u32[]{:S(2)}, u32[]{:S(2)}) collective-permute-start(f32[384,256]{1,0:T(8,128)S(1)} %add.257), channel_id=1, source_target_pairs={{0,8},{1,73},{2,10},{3,75},{4,12},{5,77},{6,14},{7,79},{8,64},{9,1... | collective-permute-start | bytes 1179656 | tf_op jit(solution)/shard_map/ppermute | solution.py:42
  87.0 11.5 %collective-permute-start.22 = (f32[2,384,256]{2,1,0:T(8,128)}, f32[2,384,256]{2,1,0:T(8,128)}, u32[]{:S(2)}, u32[]{:S(2)}) collective-permute-start(f32[2,384,256]{2,1,0:T(8,128)} %bitcast_dynamic-update-slice_fusion), channel_id=1, source_target_pairs={{0,8},{1,73},{2,10},{3,75},{4,12},{5,77},{6,14},{7,79},{8,64},{9,1... | collective-permute-start | bytes 2359304 | tf_op jit(solution)/shard_map/ppermute | solution.py:42
  100.0 4.8 %collective-permute-start.24 = (f32[96,256]{1,0:T(8,128)S(1)}, f32[96,256]{1,0:T(8,128)S(1)}, u32[]{:S(2)}, u32[]{:S(2)}) collective-permute-start(f32[96,256]{1,0:T(8,128)S(1)} %dynamic-slice_bitcast_fusion.4), channel_id=1, source_target_pairs={{0,1},{1,0},{2,3},{3,2},{4,5},{5,4},{6,7},{7,6},{8,9},{9,8},{10,11... | collective-permute-start | bytes 294920 | tf_op jit(solution)/shard_map/ppermute | solution.py:42
  103.8 3.2 %collective-permute-start.23 = (f32[2,96,256]{2,1,0:T(8,128)S(1)}, f32[2,96,256]{2,1,0:T(8,128)S(1)}, u32[]{:S(2)}, u32[]{:S(2)}) collective-permute-start(f32[2,96,256]{2,1,0:T(8,128)S(1)} %dynamic-slice_bitcast_fusion.2), channel_id=1, source_target_pairs={{0,1},{1,0},{2,3},{3,2},{4,5},{5,4},{6,7},{7,6},{8,9},{9,8},{10,11... | collective-permute-start | bytes 589832 | tf_op jit(solution)/shard_map/ppermute | solution.py:42
  104.8 3.9 %collective-permute-start.25 = (f32[96,256]{1,0:T(8,128)S(1)}, f32[96,256]{1,0:T(8,128)S(1)}, u32[]{:S(2)}, u32[]{:S(2)}) collective-permute-start(f32[96,256]{1,0:T(8,128)S(1)} %bitcast_add_fusion.3), channel_id=1, source_target_pairs={{0,16},{1,49},{2,18},{3,51},{4,20},{5,53},{6,22},{7,55},{8,24},{9,... | collective-permute-start | bytes 294920 | tf_op jit(solution)/shard_map/ppermute | solution.py:42
  109.3 13.8 %collective-permute-start.26 = (f32[2,96,256]{2,1,0:T(8,128)}, f32[2,96,256]{2,1,0:T(8,128)}, u32[]{:S(2)}, u32[]{:S(2)}) collective-permute-start(f32[2,96,256]{2,1,0:T(8,128)} %bitcast_dynamic-update-slice_fusion.5), channel_id=1, source_target_pairs={{0,16},{1,49},{2,18},{3,51},{4,20},{5,53},{6,22},{7,55},{8,24},{9,... | collective-permute-start | bytes 589832 | tf_op jit(solution)/shard_map/ppermute | solution.py:42
  116.8 19.9 %collective-permute-start.17 = (bf16[4,1,128,256]{3,2,1,0:T(8,128)(2,1)}, bf16[4,1,128,256]{3,2,1,0:T(8,128)(2,1)}, u32[]{:S(2)}, u32[]{:S(2)}) collective-permute-start(bf16[4,1,128,256]{3,2,1,0:T(8,128)(2,1)} %get-tuple-element.21), channel_id=1, source_target_pairs={{0,1},{1,0},{2,3},{3,2},{4,5},{5,4},{6,7},{7,6},{8,9},{9,8},{10,11... | collective-permute-start | bytes 786440 | tf_op jit(solution)/shard_map/ppermute | solution.py:42
  117.7 19.0 %collective-permute-start.18 = (bf16[4,1,128,256]{3,2,1,0:T(8,128)(2,1)S(1)}, bf16[4,1,128,256]{3,2,1,0:T(8,128)(2,1)}, u32[]{:S(2)}, u32[]{:S(2)}) collective-permute-start(bf16[4,1,128,256]{3,2,1,0:T(8,128)(2,1)S(1)} %get-tuple-element.22), channel_id=1, source_target_pairs={{1,2},{2,1},{3,4},{4,3},{5,6},{6,5},{7,8},{8,7},{9,10},{10,9},{11,... | collective-permute-start | bytes 786440 | tf_op jit(solution)/shard_map/ppermute | solution.py:132
  119.1 38.1 %collective-permute-start.16 = (bf16[2,8,128,256]{3,2,1,0:T(8,128)(2,1)}, bf16[2,8,128,256]{3,2,1,0:T(8,128)(2,1)S(1)}, u32[]{:S(2)}, u32[]{:S(2)}) collective-permute-start(bf16[2,8,128,256]{3,2,1,0:T(8,128)(2,1)} %slice.23), channel_id=1, source_target_pairs={{0,16},{16,32},{32,48},{48,64},{64,80},{80,96},{96,112},{1,17},{17... | collective-permute-start | bytes 3145736 | tf_op jit(solution)/shard_map/ppermute | solution.py:146
  127.2 2.7 %collective-permute-start.28 = (f32[24,256]{1,0:T(8,128)S(1)}, f32[24,256]{1,0:T(8,128)S(1)}, u32[]{:S(2)}, u32[]{:S(2)}) collective-permute-start(f32[24,256]{1,0:T(8,128)S(1)} %fusion.9), channel_id=1, source_target_pairs={{0,1},{1,0},{2,3},{3,2},{4,5},{5,4},{6,7},{7,6},{8,9},{9,8},{10,11... | collective-permute-start | bytes 73736 | tf_op jit(solution)/shard_map/ppermute | solution.py:42
  129.8 2.1 %collective-permute-start.27 = (f32[2,24,256]{2,1,0:T(8,128)S(1)}, f32[2,24,256]{2,1,0:T(8,128)S(1)}, u32[]{:S(2)}, u32[]{:S(2)}) collective-permute-start(f32[2,24,256]{2,1,0:T(8,128)S(1)} %fusion.7), channel_id=1, source_target_pairs={{0,1},{1,0},{2,3},{3,2},{4,5},{5,4},{6,7},{7,6},{8,9},{9,8},{10,11... | collective-permute-start | bytes 147464 | tf_op jit(solution)/shard_map/ppermute | solution.py:42
  130.7 6.0 %collective-permute-start.29 = (f32[24,256]{1,0:T(8,128)S(1)}, f32[24,256]{1,0:T(8,128)S(1)}, u32[]{:S(2)}, u32[]{:S(2)}) collective-permute-start(f32[24,256]{1,0:T(8,128)S(1)} %fusion.12), channel_id=1, source_target_pairs={{0,2},{1,7},{2,4},{3,1},{4,6},{5,3},{6,0},{7,5},{8,10},{9,15},{10,... | collective-permute-start | bytes 73736 | tf_op jit(solution)/shard_map/ppermute | solution.py:42
  136.7 15.8 %collective-permute-start.30 = (f32[2,24,256]{2,1,0:T(8,128)S(1)}, f32[2,24,256]{2,1,0:T(8,128)S(1)}, u32[]{:S(2)}, u32[]{:S(2)}) collective-permute-start(f32[2,24,256]{2,1,0:T(8,128)S(1)} %bitcast_dynamic-update-slice_fusion.10), channel_id=1, source_target_pairs={{0,2},{1,7},{2,4},{3,1},{4,6},{5,3},{6,0},{7,5},{8,10},{9,15},{10,... | collective-permute-start | bytes 147464 | tf_op jit(solution)/shard_map/ppermute | solution.py:42
  152.6 8.5 %collective-permute-start.31 = (f32[24,256]{1,0:T(8,128)S(1)}, f32[24,256]{1,0:T(8,128)S(1)}, u32[]{:S(2)}, u32[]{:S(2)}) collective-permute-start(f32[24,256]{1,0:T(8,128)S(1)} %dynamic-slice_bitcast_fusion.6), channel_id=1, source_target_pairs={{0,1},{1,0},{2,3},{3,2},{4,5},{5,4},{6,7},{7,6},{8,9},{9,8},{10,11... | collective-permute-start | bytes 73736 | tf_op jit(solution)/shard_map/ppermute | solution.py:42
  (15 other events, 102.0 us)
where the time goes:
time: 163 us; the launch traced here: 162 us
  starting transfers between devices  53.9 us (33%)
  Pallas kernels  39.5 us (24%)
  waiting for transfers between devices  38 us (23%)
  local copies, waits for them, and re-layouts  18.5 us (11%)
  other arithmetic  11.1 us (7%)
    ppermute x28, starting transfers between devices, moved(): return lax.ppermute(value, AXES, ring(axis))  42.8 us
    ppermute x28, waiting for transfers between devices, moved(): return lax.ppermute(value, AXES, ring(axis))  34.8 us
    pallas_call x4, Pallas kernels, part_of(): call(body, count, in_specs, frame_spec(out.shape, lambda f: f + base), ou...  18 us
    pallas_call x1, Pallas kernels, residual_block(): call(forward_kernel, n_frames, [frame_spec(wide)] + cot_specs(0) + [whole...  10.3 us
    pallas_call x1, Pallas kernels, residual_block(): call(weights_kernel, n_frames, [frame_spec(wide), frame_spec(shape), fram...  10.1 us
    ppermute x2, starting transfers between devices, along_frames(): return lax.ppermute(value, 'tm', pairs)  9 us
    unnamed x30, local copies, waits for them, and re-layouts  8.72 us
  transfers between devices with their start and end apart: 32, of which 14 were waited for; matrix products, arithmetic and copies ran while one was open for 10% of the time, Pallas kernels for 12%

commit v1 on v0

--- a/solution.py
+++ b/solution.py
@@ -4,12 +4,14 @@
 from jax import lax
 from jax.experimental import pallas as pl
 from jax.experimental.pallas import tpu as pltpu
+from jax.sharding import Mesh
 from jax.sharding import PartitionSpec as P
 
 
 epsilon = 1e-06
 F32, BF16 = jnp.float32, jnp.bfloat16
-AXES = ("tm", "rows")
+FRAME_AXES, ROW_AXES = ("y_hi", "z"), ("y_lo", "x", "core")
+AXES = FRAME_AXES + ROW_AXES
 
 
 def place(d):
@@ -67,22 +69,11 @@
 
 def scattered_ring(own, send_half, keep_half, send_full, keep_full, axis, core):
     half = keep_half + moved(send_half, "core")
+    passed = moved(half, axis)
+    mine = (lax.broadcasted_iota(jnp.int32, (2, 1, 1), 0) == core)
     full = keep_full + moved(send_full, "core")
-    passed = moved(half, axis)
-    full = put(full, take(full, core) + passed, core)
-    return own + moved(full, axis)
-
-
-def ring_blocks(value, mine, core):
-    way = 1 - 2 * core
-    opposite = take(value, (mine + 2) % 4)
-    return (
-        take(value, mine),
-        take(opposite, 1 - core),
-        take(opposite, core),
-        take(value, (mine - way) % 4),
-        take(value, (mine + way) % 4),
-    )
+    full = (full + jnp.where(mine, passed[None], 0.0)).astype(BF16)
+    return own + moved(full, axis).astype(F32)
 
 
 def both_kernels(spatial, temporal, at):
@@ -107,29 +98,30 @@
 
 
 def summed_kernels(blocks, rows_s, rows_t, at):
-    _, z, x, c = at
+    _, _, _, c = at
     chans = blocks[0].shape[-1]
     rows = 8 * (rows_s + rows_t)
-    total = scattered_ring(*blocks, "y", c)
-    total = total.reshape(4, 2, rows // 2, chans)
-    total = scattered_ring(*ring_blocks(total, z, c), "z", c).reshape(rows, chans)
+    total = scattered_ring(*blocks, "y", c).reshape(4, rows, chans)
     total = jnp.concatenate(
         [
-            total[: 8 * rows_s].reshape(4, 2, rows_s, chans),
-            total[8 * rows_s :].reshape(4, 2, rows_t, chans),
+            total[:, : 8 * rows_s].reshape(4, 4, 2, rows_s, chans),
+            total[:, 8 * rows_s :].reshape(4, 4, 2, rows_t, chans),
         ],
-        axis=2,
-    )
-    total = scattered_ring(*ring_blocks(total, x, c), "x", c)
-    mine = take(total, c) + moved(take(total, 1 - c), "core")
+        axis=3,
+    )
+    keep = lax.dynamic_index_in_dim(total, c, 2, keepdims=False)
+    send = lax.dynamic_index_in_dim(total, 1 - c, 2, keepdims=False)
+    total = (keep + moved(send, "core")).reshape(16, rows_s + rows_t, chans)
+    total = lax.all_to_all(total, ("z", "x"), split_axis=0, concat_axis=0, tiled=True)
+    mine = jnp.sum(total, axis=0)
     return mine[:rows_s], mine[rows_s:]
 
 
 def traded_edges(inner, outer):
-    count = lax.axis_size("rows")
+    count = lax.axis_size(ROW_AXES)
     pairs = [(r, r + (1 if r % 2 else -1)) for r in range(count)]
     pairs = [(r, s) for r, s in pairs if 0 <= s < count]
-    outer = lax.ppermute(outer, "rows", pairs)
+    outer = lax.ppermute(outer, ROW_AXES, pairs)
     return moved(inner, "core"), outer
 
 
@@ -141,9 +133,9 @@
 
 
 def along_frames(value, by):
-    count = lax.axis_size("tm")
+    count = lax.axis_size(FRAME_AXES)
     pairs = [(i, i + by) for i in range(count) if 0 <= i + by < count]
-    return lax.ppermute(value, "tm", pairs)
+    return lax.ppermute(value, FRAME_AXES, pairs)
 
 
 def sigmoid(value):
@@ -406,8 +398,9 @@
 
 def residual_block(video, spatial_weight, temporal_weight, cotangent):
     _, n_frames, n_rows, n_cols, chans = video.shape
-    t, r = lax.axis_index("tm"), lax.axis_index("rows")
-    y, z, x, core = at = ((t // 4) * 2 + r // 8, t % 4, (r // 2) % 4, r % 2)
+    z, x, core = (lax.axis_index(axis) for axis in ("z", "x", "core"))
+    y = lax.axis_index("y_hi") * 2 + lax.axis_index("y_lo")
+    at = (y, z, x, core)
     video, cot = video[0], cotangent[0]
     shape = (n_frames, n_rows, n_cols, chans)
     wide = (n_frames, n_rows + 2, n_cols, 3 * chans)
@@ -501,17 +494,18 @@
         3 * pair,
     )
     spatial_part, temporal_part = summed_kernels(blocks, rows_s, rows_t, at)
-    total_cells = n_frames * n_rows * n_cols * lax.axis_size("tm") * lax.axis_size("rows")
+    total_cells = n_frames * n_rows * n_cols * lax.axis_size(AXES)
     factor = float(total_cells) ** (-0.5)
     return (output[None], grad_video[None], spatial_part * factor, temporal_part * factor)
 
 
 def solution(mesh):
-    cells = P(None, "tm", "rows", None, None)
-    kernels = P(("tm", "rows"), None)
+    fine = Mesh(mesh.devices.reshape(2, 4, 2, 4, 2), AXES)
+    cells = P(None, FRAME_AXES, ROW_AXES, None, None)
+    kernels = P(AXES, None)
     return jax.shard_map(
         residual_block,
-        mesh=mesh,
+        mesh=fine,
         in_specs=(cells, kernels, kernels, cells),
         out_specs=(cells, cells, kernels, kernels),
         check_vma=False,

time: 163 us -> 149 us (0.914)
  the two profiles are of different devices: /device:TPU:47 before, /device:TPU:16 now
where the time goes in v1:
time: 149 us; the launch traced here: 148 us
  waiting for transfers between devices  55 us (37%)
  Pallas kernels  39.4 us (26%)
  starting transfers between devices  36 us (24%)
  local copies, waits for them, and re-layouts  12.1 us (8%)
  other arithmetic  4.64 us (3%)
    ppermute x20, waiting for transfers between devices, moved(): return lax.ppermute(value, AXES, ring(axis))  35.6 us
    ppermute x2, waiting for transfers between devices, along_frames(): return lax.ppermute(value, FRAME_AXES, pairs)  19.4 us
    pallas_call x4, Pallas kernels, part_of(): call(body, count, in_specs, frame_spec(out.shape, lambda f: f + base), ou...  18 us
    ppermute x20, starting transfers between devices, moved(): return lax.ppermute(value, AXES, ring(axis))  17.5 us
    pallas_call x1, Pallas kernels, residual_block(): call(forward_kernel, n_frames, [frame_spec(wide)] + cot_specs(0) + [whole...  10.3 us
    pallas_call x1, Pallas kernels, residual_block(): call(weights_kernel, n_frames, [frame_spec(wide), frame_spec(shape), fram...  10.1 us
    all_to_all x1, starting transfers between devices, summed_kernels(): lax.all_to_all(total, ('z', 'x'), split_axis=0, concat_axis=0, tiled=True)  8.31 us
    ppermute x2, starting transfers between devices, along_frames(): return lax.ppermute(value, FRAME_AXES, pairs)  8.16 us
  transfers between devices with their start and end apart: 25, of which 14 were waited for; matrix products, arithmetic and copies ran while one was open for 4% of the time, Pallas kernels for 13%

profile of v1, /device:TPU:16, one launch (start us, length us, event | category | flops | bytes accessed | tf_op | source)
XLA Modules:
  0.0 148.3 jit_solution(3059377835635733839)
XLA Ops:
  1.6 1.9 %dynamic-slice_bitcast_fusion = (bf16[4,1,128,256]{3,2,1,0:T(8,128)(2,1)}, bf16[4,1,128,256]{3,2,1,0:T(8,128)(2,1)}) fusion(bf16[1,4,8,128,256]{4,3,2,1,0:T(8,128)(2,1)} %param.5, s32[]{:T(128)S(6)} %select_n.116, s32[]{:T(128)S(6)} %select_n.115), kind=kLoop, calls=%fused_computation.13 | loop fusion | bytes 1048584 | tf_op jit(solution)/shard_map/dynamic_slice | solution.py:131
  4.7 2.0 %collective-permute-start.4 = (bf16[2,24,256]{2,1,0:T(8,128)(2,1)S(1)}, bf16[2,24,256]{2,1,0:T(8,128)(2,1)S(1)}, u32[]{:S(2)}, u32[]{:S(2)}) collective-permute-start(bf16[2,24,256]{2,1,0:T(8,128)(2,1)S(1)} %bitcast_dynamic-update-slice_fusion.13), channel_id=1, source_target_pairs={{0,16},{1,49},{2,18},{3,51},{4,20},{5,53},{6,22},{7,55},{8,24},{9,... | collective-permute-start | bytes 73736 | tf_op jit(solution)/shard_map/ppermute | solution.py:44
  6.7 3.9 %collective-permute-done.4 = bf16[2,24,256]{2,1,0:T(8,128)(2,1)S(1)} collective-permute-done((bf16[2,24,256]{2,1,0:T(8,128)(2,1)S(1)}, bf16[2,24,256]{2,1,0:T(8,128)(2,1)S(1)}, u32[]{:S(2)}, u32[]{:S(2)}) %collective-permute-start.4) | collective-permute-done | bytes 24608 | tf_op jit(solution)/shard_map/ppermute | solution.py:44
  10.6 4.6 %collective-permute-start.5 = (bf16[2,24,256]{2,1,0:T(8,128)(2,1)S(1)}, bf16[2,24,256]{2,1,0:T(8,128)(2,1)S(1)}, u32[]{:S(2)}, u32[]{:S(2)}) collective-permute-start(bf16[2,24,256]{2,1,0:T(8,128)(2,1)S(1)} %collective-permute-done.4), channel_id=1, source_target_pairs={{0,1},{1,0},{2,3},{3,2},{4,5},{5,4},{6,7},{7,6},{8,9},{9,8},{10,11... | collective-permute-start | bytes 73736 | tf_op jit(solution)/shard_map/ppermute | solution.py:44
  16.9 4.9 %collective-permute-start.8 = (bf16[2,96,256]{2,1,0:T(8,128)(2,1)S(1)}, bf16[2,96,256]{2,1,0:T(8,128)(2,1)S(1)}, u32[]{:S(2)}, u32[]{:S(2)}) collective-permute-start(bf16[2,96,256]{2,1,0:T(8,128)(2,1)S(1)} %bitcast.83), channel_id=1, source_target_pairs={{0,8},{1,73},{2,10},{3,75},{4,12},{5,77},{6,14},{7,79},{8,64},{9,1... | collective-permute-start | bytes 294920 | tf_op jit(solution)/shard_map/ppermute | solution.py:44
  21.9 2.2 %collective-permute-done.8 = bf16[2,96,256]{2,1,0:T(8,128)(2,1)S(1)} collective-permute-done((bf16[2,96,256]{2,1,0:T(8,128)(2,1)S(1)}, bf16[2,96,256]{2,1,0:T(8,128)(2,1)S(1)}, u32[]{:S(2)}, u32[]{:S(2)}) %collective-permute-start.8) | collective-permute-done | bytes 98336 | tf_op jit(solution)/shard_map/ppermute | solution.py:44
  24.0 2.4 %collective-permute-start.10 = (bf16[96,256]{1,0:T(8,128)(2,1)S(1)}, bf16[96,256]{1,0:T(8,128)(2,1)S(1)}, u32[]{:S(2)}, u32[]{:S(2)}) collective-permute-start(bf16[96,256]{1,0:T(8,128)(2,1)S(1)} %dynamic-slice_bitcast_fusion.3), channel_id=1, source_target_pairs={{0,8},{1,73},{2,10},{3,75},{4,12},{5,77},{6,14},{7,79},{8,64},{9,1... | collective-permute-start | bytes 147464 | tf_op jit(solution)/shard_map/ppermute | solution.py:44
  26.4 1.7 %collective-permute-done.10 = bf16[96,256]{1,0:T(8,128)(2,1)S(1)} collective-permute-done((bf16[96,256]{1,0:T(8,128)(2,1)S(1)}, bf16[96,256]{1,0:T(8,128)(2,1)S(1)}, u32[]{:S(2)}, u32[]{:S(2)}) %collective-permute-start.10) | collective-permute-done | bytes 49184 | tf_op jit(solution)/shard_map/ppermute | solution.py:44
  28.2 1.2 collective-permute-done.11
  30.6 6.3 %collective-permute-start.2 = (bf16[2,8,128,256]{3,2,1,0:T(8,128)(2,1)}, bf16[2,8,128,256]{3,2,1,0:T(8,128)(2,1)}, u32[]{:S(2)}, u32[]{:S(2)}) collective-permute-start(bf16[2,8,128,256]{3,2,1,0:T(8,128)(2,1)} %slice_bitcast_fusion), channel_id=1, source_target_pairs={{16,0},{32,16},{48,32},{64,48},{80,64},{96,80},{112,96},{17,1},{33... | collective-permute-start | bytes 3145736 | tf_op jit(solution)/shard_map/ppermute | solution.py:138
  37.2 1.2 collective-permute-done.12
  38.4 2.2 %shard_map.84._ = bf16[4,10,128,768]{3,2,1,0:T(8,128)(2,1)S(1)} custom-call(s32[4]{0:T(128)S(1)} %get-tuple-element.35.at, bf16[4,8,128,256]{3,2,1,0:T(8,128)(2,1)S(1)} %bitcast.62, bf16[4,1,128,256]{3,2,1,0:T(8,128)(2,1)S(1)} %collective-permute-done.inner, bf16[4,1,128,256]{3,2,1,0:T(8,128)(2,1)S(1)} %collective-permute-done.1.outer, s32[1]{0:T(128)} %constant.105.clone.1._), custom_call_target="tpu_custom_call" | custom-call | flops 268435456 | bytes 8388608 | tf_op jit(solution)/shard_map/pallas_call | solution.py:375
  40.6 2.2 %shard_map.85.shifts = bf16[4,10,128,768]{3,2,1,0:T(8,128)(2,1)S(1)} custom-call(s32[4]{0:T(128)S(1)} %get-tuple-element.34.at, bf16[4,8,128,256]{3,2,1,0:T(8,128)(2,1)S(1)} %bitcast.63, bf16[4,1,128,256]{3,2,1,0:T(8,128)(2,1)S(1)} %collective-permute-done.inner, ...), custom_call_target="tpu_custom_call", output_to_operand_aliasing={{}: (4, {})} | custom-call | flops 268435456 | bytes 8388608 | tf_op jit(solution)/shard_map/pallas_call | solution.py:375
  43.0 6.8 %collective-permute-done.14 = bf16[384,256]{1,0:T(8,128)(2,1)S(1)} collective-permute-done((bf16[384,256]{1,0:T(8,128)(2,1)S(1)}, bf16[384,256]{1,0:T(8,128)(2,1)S(1)}, u32[]{:S(2)}, u32[]{:S(2)}) %collective-permute-start.14) | collective-permute-done | bytes 196640 | tf_op jit(solution)/shard_map/ppermute | solution.py:44
  49.9 1.4 collective-permute-done.15
  51.9 8.6 %collective-permute-done.2.ahead1.ahead2 = bf16[2,8,128,256]{3,2,1,0:T(8,128)(2,1)} collective-permute-done((bf16[2,8,128,256]{3,2,1,0:T(8,128)(2,1)}, bf16[2,8,128,256]{3,2,1,0:T(8,128)(2,1)}, u32[]{:S(2)}, u32[]{:S(2)}) %collective-permute-start.2) | collective-permute-done | bytes 1048608 | tf_op jit(solution)/shard_map/ppermute | solution.py:138
  60.5 10.3 %shard_map.87 = (bf16[4,8,128,256]{3,2,1,0:T(8,128)(2,1)S(1)}, bf16[4,8,128,256]{3,2,1,0:T(8,128)(2,1)S(1)}, bf16[4,1,128,256]{3,2,1,0:T(8,128)(2,1)}, bf16[4,1,128,256]{3,2,1,0:T(8,128)(2,1)}) custom-call(s32[4]{0:T(128)S(1)} %get-tuple-element.35.at, bf16[4,10,128,768]{3,2,1,0:T(8,128)(2,1)S(1)} %shard_map.85.shifts, ...), custom_call_target="tpu_custom_call" | custom-call | flops 6442450944 | bytes 8388608 | tf_op jit(solution)/shard_map/pallas_call | solution.py:445
  70.8 10.1 %shard_map.91 = (f32[2,384,256]{2,1,0:T(8,128)S(1)}, f32[384,256]{1,0:T(8,128)S(1)}, f32[384,256]{1,0:T(8,128)S(1)}, f32[2,384,256]{2,1,0:T(8,128)S(1)}, f32[2,384,256]{2,1,0:T(8,128)S(1)}) custom-call(s32[4]{0:T(128)S(1)} %get-tuple-element.35.at, bf16[4,10,128,768]{3,2,1,0:T(8,128)(2,1)S(1)} %shard_map.85.shifts, ...), custom_call_target="tpu_custom_call" | custom-call | flops 6442450944 | bytes 8388608 | tf_op jit(solution)/shard_map/pallas_call | solution.py:458
  81.8 1.2 collective-permute-done.20
  83.4 7.5 %collective-permute-done.21 = f32[384,256]{1,0:T(8,128)S(1)} collective-permute-done((f32[384,256]{1,0:T(8,128)S(1)}, f32[384,256]{1,0:T(8,128)S(1)}, u32[]{:S(2)}, u32[]{:S(2)}) %collective-permute-start.21) | collective-permute-done | bytes 393248 | tf_op jit(solution)/shard_map/ppermute | solution.py:44
  91.6 7.4 %collective-permute-done.22 = bf16[2,384,256]{2,1,0:T(8,128)(2,1)S(1)} collective-permute-done((bf16[2,384,256]{2,1,0:T(8,128)(2,1)S(1)}, bf16[2,384,256]{2,1,0:T(8,128)(2,1)S(1)}, u32[]{:S(2)}, u32[]{:S(2)}) %collective-permute-start.22) | collective-permute-done | bytes 393248 | tf_op jit(solution)/shard_map/ppermute | solution.py:44
  100.1 1.0 slice.23
  101.1 1.9 %collective-permute-start.16 = (bf16[2,8,128,256]{3,2,1,0:T(8,128)(2,1)}, bf16[2,8,128,256]{3,2,1,0:T(8,128)(2,1)S(1)}, u32[]{:S(2)}, u32[]{:S(2)}) collective-permute-start(bf16[2,8,128,256]{3,2,1,0:T(8,128)(2,1)} %slice.23), channel_id=1, source_target_pairs={{0,16},{16,32},{32,48},{48,64},{64,80},{80,96},{96,112},{1,17},{17... | collective-permute-start | bytes 3145736 | tf_op jit(solution)/shard_map/ppermute | solution.py:138
  103.6 1.4 collective-permute-start.18
  107.2 8.3 %all-to-all-start = ((f32[16,24,256]{2,1,0:T(8,128)}), f32[16,24,256]{2,1,0:T(8,128)}, u32[]{:S(2)}, u32[]{:S(2)}) async-start(f32[16,24,256]{2,1,0:T(8,128)} %bitcast.78), calls=%async_computation | async-start | bytes 786432 | tf_op jit(solution)/shard_map/all_to_all | solution.py:115
  115.5 1.6 %copy-done.1 = bf16[1,4,8,128,256]{4,3,2,1,0:T(8,128)(2,1)S(1)} copy-done((bf16[1,4,8,128,256]{4,3,2,1,0:T(8,128)(2,1)S(1)}, bf16[1,4,8,128,256]{4,3,2,1,0:T(8,128)(2,1)}, u32[]{:S(2)}) %copy-start.1) | copy-done | bytes 2097176
  117.1 1.3 copy-done.3
  118.4 1.6 %copy-done.6 = bf16[1,4,8,128,256]{4,3,2,1,0:T(8,128)(2,1)S(1)} copy-done((bf16[1,4,8,128,256]{4,3,2,1,0:T(8,128)(2,1)S(1)}, bf16[1,4,8,128,256]{4,3,2,1,0:T(8,128)(2,1)}, u32[]{:S(2)}) %copy-start.6) | copy-done | bytes 2097176
  120.0 1.6 %copy-done.9 = bf16[4,8,128,256]{3,2,1,0:T(8,128)(2,1)S(1)} copy-done((bf16[4,8,128,256]{3,2,1,0:T(8,128)(2,1)S(1)}, bf16[4,8,128,256]{3,2,1,0:T(8,128)(2,1)}, u32[]{:S(2)}) %copy-start.9) | copy-done | bytes 2097176
  121.6 9.8 %shard_map.90 = bf16[4,8,128,256]{3,2,1,0:T(8,128)(2,1)} custom-call(s32[4]{0:T(128)S(1)} %get-tuple-element.35.at, bf16[4,8,128,256]{3,2,1,0:T(8,128)(2,1)S(1)} %copy-done.9, bf16[4,1,128,256]{3,2,1,0:T(8,128)(2,1)} %collective-permute-done.17.inner, bf16[4,1,128,256]{3,2,1,0:T(8,128)(2,1)} %collective-permute-done.18.outer, ...), custom_call_target="tpu_custom_call" | custom-call | flops 4831838208 | bytes 8388608 | tf_op jit(solution)/shard_map/pallas_call | solution.py:375
  131.3 10.8 %collective-permute-done.16.past0.past1 = bf16[2,8,128,256]{3,2,1,0:T(8,128)(2,1)S(1)} collective-permute-done((bf16[2,8,128,256]{3,2,1,0:T(8,128)(2,1)}, bf16[2,8,128,256]{3,2,1,0:T(8,128)(2,1)S(1)}, u32[]{:S(2)}, u32[]{:S(2)}) %collective-permute-start.16) | collective-permute-done | bytes 1048608 | tf_op jit(solution)/shard_map/ppermute | solution.py:138
  142.1 3.9 %shard_map.88 = bf16[4,8,128,256]{3,2,1,0:T(8,128)(2,1)} custom-call(s32[4]{0:T(128)S(1)} %get-tuple-element.35.at, bf16[4,8,128,256]{3,2,1,0:T(8,128)(2,1)S(1)} %bitcast.65, bf16[2,8,128,256]{3,2,1,0:T(8,128)(2,1)S(1)} %collective-permute-done.16.past0.past1, bf16[2,8,128,256]{3,2,1,0:T(8,128)(2,1)S(1)} %collective-permute-done.16.past0.past1, ...), custom_call_target="tpu_custom_call" | custom-call | flops 1610612736 | bytes 8388608 | tf_op jit(solution)/shard_map/pallas_call | solution.py:375
  (88 shorter events, 14.1 us)
Async XLA Ops:
  0.6 28.9 %copy-start.4 = (bf16[1,4,8,128,256]{4,3,2,1,0:T(8,128)(2,1)S(1)}, bf16[1,4,8,128,256]{4,3,2,1,0:T(8,128)(2,1)}, u32[]{:S(2)}) copy-start(bf16[1,4,8,128,256]{4,3,2,1,0:T(8,128)(2,1)} %param.8) | copy-start | bytes 6291460
  1.5 3.1 %collective-permute-start.3 = (bf16[24,256]{1,0:T(8,128)(2,1)S(1)}, bf16[24,256]{1,0:T(8,128)(2,1)S(1)}, u32[]{:S(2)}, u32[]{:S(2)}) collective-permute-start(bf16[24,256]{1,0:T(8,128)(2,1)S(1)} %get-tuple-element.29), channel_id=1, source_target_pairs={{0,1},{1,0},{2,3},{3,2},{4,5},{5,4},{6,7},{7,6},{8,9},{9,8},{10,11... | collective-permute-start | bytes 36872 | tf_op jit(solution)/shard_map/ppermute | solution.py:44
  3.4 35.0 %collective-permute-start = (bf16[4,1,128,256]{3,2,1,0:T(8,128)(2,1)}, bf16[4,1,128,256]{3,2,1,0:T(8,128)(2,1)S(1)}, u32[]{:S(2)}, u32[]{:S(2)}) collective-permute-start(bf16[4,1,128,256]{3,2,1,0:T(8,128)(2,1)} %get-tuple-element.31), channel_id=1, source_target_pairs={{0,1},{1,0},{2,3},{3,2},{4,5},{5,4},{6,7},{7,6},{8,9},{9,8},{10,11... | collective-permute-start | bytes 786440 | tf_op jit(solution)/shard_map/ppermute | solution.py:44
  3.9 34.5 %collective-permute-start.1 = (bf16[4,1,128,256]{3,2,1,0:T(8,128)(2,1)}, bf16[4,1,128,256]{3,2,1,0:T(8,128)(2,1)S(1)}, u32[]{:S(2)}, u32[]{:S(2)}) collective-permute-start(bf16[4,1,128,256]{3,2,1,0:T(8,128)(2,1)} %get-tuple-element.30), channel_id=1, source_target_pairs={{1,2},{2,1},{3,4},{4,3},{5,6},{6,5},{7,8},{8,7},{9,10},{10,9},{11,... | collective-permute-start | bytes 786440 | tf_op jit(solution)/shard_map/ppermute | solution.py:124
  4.7 5.9 %collective-permute-start.4 = (bf16[2,24,256]{2,1,0:T(8,128)(2,1)S(1)}, bf16[2,24,256]{2,1,0:T(8,128)(2,1)S(1)}, u32[]{:S(2)}, u32[]{:S(2)}) collective-permute-start(bf16[2,24,256]{2,1,0:T(8,128)(2,1)S(1)} %bitcast_dynamic-update-slice_fusion.13), channel_id=1, source_target_pairs={{0,16},{1,49},{2,18},{3,51},{4,20},{5,53},{6,22},{7,55},{8,24},{9,... | collective-permute-start | bytes 73736 | tf_op jit(solution)/shard_map/ppermute | solution.py:44
  10.6 4.9 %collective-permute-start.6 = (bf16[24,256]{1,0:T(8,128)(2,1)S(1)}, bf16[24,256]{1,0:T(8,128)(2,1)S(1)}, u32[]{:S(2)}, u32[]{:S(2)}) collective-permute-start(bf16[24,256]{1,0:T(8,128)(2,1)S(1)} %dynamic-slice_bitcast_fusion.4), channel_id=1, source_target_pairs={{0,16},{1,49},{2,18},{3,51},{4,20},{5,53},{6,22},{7,55},{8,24},{9,... | collective-permute-start | bytes 36872 | tf_op jit(solution)/shard_map/ppermute | solution.py:44
  10.6 5.5 %collective-permute-start.5 = (bf16[2,24,256]{2,1,0:T(8,128)(2,1)S(1)}, bf16[2,24,256]{2,1,0:T(8,128)(2,1)S(1)}, u32[]{:S(2)}, u32[]{:S(2)}) collective-permute-start(bf16[2,24,256]{2,1,0:T(8,128)(2,1)S(1)} %collective-permute-done.4), channel_id=1, source_target_pairs={{0,1},{1,0},{2,3},{3,2},{4,5},{5,4},{6,7},{7,6},{8,9},{9,8},{10,11... | collective-permute-start | bytes 73736 | tf_op jit(solution)/shard_map/ppermute | solution.py:44
  15.5 1.4 collective-permute-start.7
  16.9 7.1 %collective-permute-start.8 = (bf16[2,96,256]{2,1,0:T(8,128)(2,1)S(1)}, bf16[2,96,256]{2,1,0:T(8,128)(2,1)S(1)}, u32[]{:S(2)}, u32[]{:S(2)}) collective-permute-start(bf16[2,96,256]{2,1,0:T(8,128)(2,1)S(1)} %bitcast.83), channel_id=1, source_target_pairs={{0,8},{1,73},{2,10},{3,75},{4,12},{5,77},{6,14},{7,79},{8,64},{9,1... | collective-permute-start | bytes 294920 | tf_op jit(solution)/shard_map/ppermute | solution.py:44
  24.0 4.2 %collective-permute-start.10 = (bf16[96,256]{1,0:T(8,128)(2,1)S(1)}, bf16[96,256]{1,0:T(8,128)(2,1)S(1)}, u32[]{:S(2)}, u32[]{:S(2)}) collective-permute-start(bf16[96,256]{1,0:T(8,128)(2,1)S(1)} %dynamic-slice_bitcast_fusion.3), channel_id=1, source_target_pairs={{0,8},{1,73},{2,10},{3,75},{4,12},{5,77},{6,14},{7,79},{8,64},{9,1... | collective-permute-start | bytes 147464 | tf_op jit(solution)/shard_map/ppermute | solution.py:44
  26.4 1.8 %collective-permute-start.9 = (bf16[2,96,256]{2,1,0:T(8,128)(2,1)S(1)}, bf16[2,96,256]{2,1,0:T(8,128)(2,1)S(1)}, u32[]{:S(2)}, u32[]{:S(2)}) collective-permute-start(bf16[2,96,256]{2,1,0:T(8,128)(2,1)S(1)} %collective-permute-done.8), channel_id=1, source_target_pairs={{0,1},{1,0},{2,3},{3,2},{4,5},{5,4},{6,7},{7,6},{8,9},{9,8},{10,11... | collective-permute-start | bytes 294920 | tf_op jit(solution)/shard_map/ppermute | solution.py:44
  28.2 1.2 collective-permute-start.11
  29.4 9.0 %collective-permute-start.12 = (bf16[2,384,256]{2,1,0:T(8,128)(2,1)S(1)}, bf16[2,384,256]{2,1,0:T(8,128)(2,1)S(1)}, u32[]{:S(2)}, u32[]{:S(2)}) collective-permute-start(bf16[2,384,256]{2,1,0:T(8,128)(2,1)S(1)} %bitcast.79), channel_id=1, source_target_pairs={{0,2},{1,7},{2,4},{3,1},{4,6},{5,3},{6,0},{7,5},{8,10},{9,15},{10,... | collective-permute-start | bytes 1179656 | tf_op jit(solution)/shard_map/ppermute | solution.py:44
  30.6 7.8 %copy-start = (bf16[1,4,8,128,256]{4,3,2,1,0:T(8,128)(2,1)S(1)}, bf16[1,4,8,128,256]{4,3,2,1,0:T(8,128)(2,1)}, u32[]{:S(2)}) copy-start(bf16[1,4,8,128,256]{4,3,2,1,0:T(8,128)(2,1)} %param.5) | copy-start | bytes 6291460
  30.6 29.9 %collective-permute-start.2 = (bf16[2,8,128,256]{3,2,1,0:T(8,128)(2,1)}, bf16[2,8,128,256]{3,2,1,0:T(8,128)(2,1)}, u32[]{:S(2)}, u32[]{:S(2)}) collective-permute-start(bf16[2,8,128,256]{3,2,1,0:T(8,128)(2,1)} %slice_bitcast_fusion), channel_id=1, source_target_pairs={{16,0},{32,16},{48,32},{64,48},{80,64},{96,80},{112,96},{17,1},{33... | collective-permute-start | bytes 3145736 | tf_op jit(solution)/shard_map/ppermute | solution.py:138
  38.4 11.4 %collective-permute-start.13 = (bf16[2,384,256]{2,1,0:T(8,128)(2,1)S(1)}, bf16[2,384,256]{2,1,0:T(8,128)(2,1)S(1)}, u32[]{:S(2)}, u32[]{:S(2)}) collective-permute-start(bf16[2,384,256]{2,1,0:T(8,128)(2,1)S(1)} %collective-permute-done.12), channel_id=1, source_target_pairs={{0,1},{1,0},{2,3},{3,2},{4,5},{5,4},{6,7},{7,6},{8,9},{9,8},{10,11... | collective-permute-start | bytes 1179656 | tf_op jit(solution)/shard_map/ppermute | solution.py:44
  42.8 8.5 %copy-start.7 = (bf16[192,192]{1,0:T(8,128)(2,1)S(1)}, bf16[192,192]{1,0:T(8,128)(2,1)}, u32[]{:S(2)}) copy-start(bf16[192,192]{1,0:T(8,128)(2,1)} %constant.118.clone.order) | copy-start | bytes 221188
  42.8 6.9 %collective-permute-start.14 = (bf16[384,256]{1,0:T(8,128)(2,1)S(1)}, bf16[384,256]{1,0:T(8,128)(2,1)S(1)}, u32[]{:S(2)}, u32[]{:S(2)}) collective-permute-start(bf16[384,256]{1,0:T(8,128)(2,1)S(1)} %dynamic-slice_bitcast_fusion.2), channel_id=1, source_target_pairs={{0,2},{1,7},{2,4},{3,1},{4,6},{5,3},{6,0},{7,5},{8,10},{9,15},{10,... | collective-permute-start | bytes 589832 | tf_op jit(solution)/shard_map/ppermute | solution.py:44
  43.0 17.5 %copy-start.5 = (bf16[1,4,8,128,256]{4,3,2,1,0:T(8,128)(2,1)S(1)}, bf16[1,4,8,128,256]{4,3,2,1,0:T(8,128)(2,1)}, u32[]{:S(2)}) copy-start(bf16[1,4,8,128,256]{4,3,2,1,0:T(8,128)(2,1)} %param.8) | copy-start | bytes 6291460
  49.8 1.4 collective-permute-start.15
  70.8 10.2 %copy-start.8 = (bf16[4,8,128,256]{3,2,1,0:T(8,128)(2,1)}, bf16[4,8,128,256]{3,2,1,0:T(8,128)(2,1)S(1)}, u32[]{:S(2)}) copy-start(bf16[4,8,128,256]{3,2,1,0:T(8,128)(2,1)S(1)} %get-tuple-element.20.grad_pre) | copy-start | bytes 6291460
  81.0 2.0 %collective-permute-start.20 = (f32[384,256]{1,0:T(8,128)S(1)}, f32[384,256]{1,0:T(8,128)S(1)}, u32[]{:S(2)}, u32[]{:S(2)}) collective-permute-start(f32[384,256]{1,0:T(8,128)S(1)} %get-tuple-element.27), channel_id=1, source_target_pairs={{0,1},{1,0},{2,3},{3,2},{4,5},{5,4},{6,7},{7,6},{8,9},{9,8},{10,11... | collective-permute-start | bytes 1179656 | tf_op jit(solution)/shard_map/ppermute | solution.py:44
  81.6 9.3 %collective-permute-start.19 = (f32[2,384,256]{2,1,0:T(8,128)S(1)}, f32[2,384,256]{2,1,0:T(8,128)S(1)}, u32[]{:S(2)}, u32[]{:S(2)}) collective-permute-start(f32[2,384,256]{2,1,0:T(8,128)S(1)} %get-tuple-element.25), channel_id=1, source_target_pairs={{0,1},{1,0},{2,3},{3,2},{4,5},{5,4},{6,7},{7,6},{8,9},{9,8},{10,11... | collective-permute-start | bytes 2359304 | tf_op jit(solution)/shard_map/ppermute | solution.py:44
  83.0 7.8 %collective-permute-start.21 = (f32[384,256]{1,0:T(8,128)S(1)}, f32[384,256]{1,0:T(8,128)S(1)}, u32[]{:S(2)}, u32[]{:S(2)}) collective-permute-start(f32[384,256]{1,0:T(8,128)S(1)} %add.170), channel_id=1, source_target_pairs={{0,8},{1,73},{2,10},{3,75},{4,12},{5,77},{6,14},{7,79},{8,64},{9,1... | collective-permute-start | bytes 1179656 | tf_op jit(solution)/shard_map/ppermute | solution.py:44
  91.1 7.8 %collective-permute-start.22 = (bf16[2,384,256]{2,1,0:T(8,128)(2,1)S(1)}, bf16[2,384,256]{2,1,0:T(8,128)(2,1)S(1)}, u32[]{:S(2)}, u32[]{:S(2)}) collective-permute-start(bf16[2,384,256]{2,1,0:T(8,128)(2,1)S(1)} %add_convert_fusion), channel_id=1, source_target_pairs={{0,8},{1,73},{2,10},{3,75},{4,12},{5,77},{6,14},{7,79},{8,64},{9,1... | collective-permute-start | bytes 1179656 | tf_op jit(solution)/shard_map/ppermute | solution.py:44
  100.0 6.4 %collective-permute-start.23 = (f32[4,4,24,256]{3,2,1,0:T(8,128)S(1)}, f32[4,4,24,256]{3,2,1,0:T(8,128)S(1)}, u32[]{:S(2)}, u32[]{:S(2)}) collective-permute-start(f32[4,4,24,256]{3,2,1,0:T(8,128)S(1)} %bitcast.82), channel_id=1, source_target_pairs={{0,1},{1,0},{2,3},{3,2},{4,5},{5,4},{6,7},{7,6},{8,9},{9,8},{10,11... | collective-permute-start | bytes 1179656 | tf_op jit(solution)/shard_map/ppermute | solution.py:44
  101.1 41.0 %collective-permute-start.16 = (bf16[2,8,128,256]{3,2,1,0:T(8,128)(2,1)}, bf16[2,8,128,256]{3,2,1,0:T(8,128)(2,1)S(1)}, u32[]{:S(2)}, u32[]{:S(2)}) collective-permute-start(bf16[2,8,128,256]{3,2,1,0:T(8,128)(2,1)} %slice.23), channel_id=1, source_target_pairs={{0,16},{16,32},{32,48},{48,64},{64,80},{80,96},{96,112},{1,17},{17... | collective-permute-start | bytes 3145736 | tf_op jit(solution)/shard_map/ppermute | solution.py:138
  103.0 12.5 %collective-permute-start.17 = (bf16[4,1,128,256]{3,2,1,0:T(8,128)(2,1)}, bf16[4,1,128,256]{3,2,1,0:T(8,128)(2,1)}, u32[]{:S(2)}, u32[]{:S(2)}) collective-permute-start(bf16[4,1,128,256]{3,2,1,0:T(8,128)(2,1)} %get-tuple-element.21), channel_id=1, source_target_pairs={{0,1},{1,0},{2,3},{3,2},{4,5},{5,4},{6,7},{7,6},{8,9},{9,8},{10,11... | collective-permute-start | bytes 786440 | tf_op jit(solution)/shard_map/ppermute | solution.py:44
  103.6 11.9 %collective-permute-start.18 = (bf16[4,1,128,256]{3,2,1,0:T(8,128)(2,1)}, bf16[4,1,128,256]{3,2,1,0:T(8,128)(2,1)}, u32[]{:S(2)}, u32[]{:S(2)}) collective-permute-start(bf16[4,1,128,256]{3,2,1,0:T(8,128)(2,1)} %get-tuple-element.22), channel_id=1, source_target_pairs={{1,2},{2,1},{3,4},{4,3},{5,6},{6,5},{7,8},{8,7},{9,10},{10,9},{11,... | collective-permute-start | bytes 786440 | tf_op jit(solution)/shard_map/ppermute | solution.py:124
  107.2 38.8 %all-to-all-start = ((f32[16,24,256]{2,1,0:T(8,128)}), f32[16,24,256]{2,1,0:T(8,128)}, u32[]{:S(2)}, u32[]{:S(2)}) async-start(f32[16,24,256]{2,1,0:T(8,128)} %bitcast.78), calls=%async_computation | async-start | bytes 786432 | tf_op jit(solution)/shard_map/all_to_all | solution.py:115
  115.5 1.6 %copy-start.1 = (bf16[1,4,8,128,256]{4,3,2,1,0:T(8,128)(2,1)S(1)}, bf16[1,4,8,128,256]{4,3,2,1,0:T(8,128)(2,1)}, u32[]{:S(2)}) copy-start(bf16[1,4,8,128,256]{4,3,2,1,0:T(8,128)(2,1)} %param.5) | copy-start | bytes 6291460
  118.4 1.6 %copy-start.6 = (bf16[1,4,8,128,256]{4,3,2,1,0:T(8,128)(2,1)S(1)}, bf16[1,4,8,128,256]{4,3,2,1,0:T(8,128)(2,1)}, u32[]{:S(2)}) copy-start(bf16[1,4,8,128,256]{4,3,2,1,0:T(8,128)(2,1)} %param.8) | copy-start | bytes 6291460
  (3 other events, 3.9 us)

commit v2 on v1

--- a/solution.py
+++ b/solution.py
@@ -12,6 +12,7 @@
 F32, BF16 = jnp.float32, jnp.bfloat16
 FRAME_AXES, ROW_AXES = ("y_hi", "z"), ("y_lo", "x", "core")
 AXES = FRAME_AXES + ROW_AXES
+UNIT_AXES = ("y_hi", "z", "y_lo")
 
 
 def place(d):
@@ -77,17 +78,15 @@
 
 
 def both_kernels(spatial, temporal, at):
-    y, z, x, c = at
-    chans = spatial.shape[1]
-    rows_s, rows_t = spatial.shape[0], temporal.shape[0]
+    x, c = at
     own = jnp.concatenate([spatial, temporal], axis=0)
-    other = moved(own, "core")
-    pair = put(put(jnp.zeros((2,) + own.shape, own.dtype), own, c), other, 1 - c)
-    rows = rows_s + rows_t
-    units = gathered_axis(pair, "z", z, c)
-    units = gathered_axis(units.reshape(2, 4 * rows, chans), "y", y, c)
-    units = gathered_axis(units.reshape(2, 16 * rows, chans), "x", x, c)
-    return units.reshape(4, 4, 4, 2 * rows, chans)
+    rows, chans = own.shape
+    copies = jnp.broadcast_to(own[None], (16, rows, chans))
+    units = lax.all_to_all(copies, UNIT_AXES, split_axis=0, concat_axis=0, tiled=True)
+    units = units.reshape(16 * rows, chans)
+    other = moved(units, "core")
+    pair = put(put(jnp.zeros((2, 16 * rows, chans), units.dtype), units, c), other, 1 - c)
+    return gathered_axis(pair, "x", x, c).reshape(4, 2, 16, rows, chans)
 
 
 def unit_order(rows_s, rows_t):
@@ -97,22 +96,13 @@
     return np.eye(8 * rows, dtype=np.float32)[source]
 
 
-def summed_kernels(blocks, rows_s, rows_t, at):
-    _, _, _, c = at
+def summed_kernels(blocks, rows_s, rows_t, core):
     chans = blocks[0].shape[-1]
-    rows = 8 * (rows_s + rows_t)
-    total = scattered_ring(*blocks, "y", c).reshape(4, rows, chans)
-    total = jnp.concatenate(
-        [
-            total[:, : 8 * rows_s].reshape(4, 4, 2, rows_s, chans),
-            total[:, 8 * rows_s :].reshape(4, 4, 2, rows_t, chans),
-        ],
-        axis=3,
-    )
-    keep = lax.dynamic_index_in_dim(total, c, 2, keepdims=False)
-    send = lax.dynamic_index_in_dim(total, 1 - c, 2, keepdims=False)
-    total = (keep + moved(send, "core")).reshape(16, rows_s + rows_t, chans)
-    total = lax.all_to_all(total, ("z", "x"), split_axis=0, concat_axis=0, tiled=True)
+    total = scattered_ring(*blocks, "x", core).reshape(16, 2, rows_s + rows_t, chans)
+    keep = lax.dynamic_index_in_dim(total, core, 1, keepdims=False)
+    send = lax.dynamic_index_in_dim(total, 1 - core, 1, keepdims=False)
+    total = keep + moved(send, "core")
+    total = lax.all_to_all(total, UNIT_AXES, split_axis=0, concat_axis=0, tiled=True)
     mine = jnp.sum(total, axis=0)
     return mine[:rows_s], mine[rows_s:]
 
@@ -181,20 +171,14 @@
         store_shifts(shifts.at[0], row, normed * sigmoid(normed))
 
 
-def unit_number(y, z):
-    return ((y // 2) * 4 + z) * 2 + y % 2
-
-
 def assemble_kernel(order, units, w_s, w_t, w_back):
     chans = w_s.shape[1]
     rows_s, rows_t = w_s.shape[0] // 16, w_t.shape[0] // 16
-    for y in range(4):
-        for z in range(4):
-            u = unit_number(y, z)
-            blocks = jnp.concatenate([units[x, y, z] for x in range(4)], axis=0)
-            unit = dot(order[...], blocks).astype(BF16)
-            w_s[rows_s * u : rows_s * (u + 1)] = unit[:rows_s]
-            w_t[rows_t * u : rows_t * (u + 1)] = unit[rows_s:]
+    for u in range(16):
+        blocks = [units[x, core, u] for x in range(4) for core in range(2)]
+        unit = dot(order[...], jnp.concatenate(blocks, axis=0)).astype(BF16)
+        w_s[rows_s * u : rows_s * (u + 1)] = unit[:rows_s]
+        w_t[rows_t * u : rows_t * (u + 1)] = unit[rows_s:]
     for k in range(3):
         w_back[chans * k : chans * (k + 1)] = w_t[chans * (2 - k) : chans * (3 - k)].T
 
@@ -243,7 +227,7 @@
 
 def weights_kernel(
     at, shifts, grad_pre, hidden, cot0, cot1, cot2, ahead1, ahead2,
-    own, send_half, keep_half, send_full, keep_full, grad_s, grad_t,
+    own, send_half, keep_half, send_full, keep_full, grad_s, grad_t, by_x,
 ):
     @pl.when(pl.program_id(0) == 0)
     def _():
@@ -265,27 +249,27 @@
 
     @pl.when(pl.program_id(0) == last)
     def _():
-        rows_s, rows_t = 9 * chans // 16, 3 * chans // 16
+        rows_s, rows_t = 9 * chans // 128, 3 * chans // 128
+        rows = rows_s + rows_t
+        for u in range(16):
+            for block in range(8):
+                x, row, number = block // 2, (2 * u + block % 2) * rows, 8 * u + block
+                by_x[x, row : row + rows] = jnp.concatenate(
+                    [
+                        grad_s[rows_s * number : rows_s * (number + 1)],
+                        grad_t[rows_t * number : rows_t * (number + 1)],
+                    ],
+                    axis=0,
+                )
         mine, core = at[0], at[1]
         way = 1 - 2 * core
-
-        def fill(out, index, y, z):
-            u = unit_number(y, z)
-            top = (index % 2) * (rows_s + rows_t)
-            at_s = pl.ds(pl.multiple_of(rows_s * u, rows_t), rows_s)
-            at_t = pl.ds(pl.multiple_of(rows_t * u, rows_t), rows_t)
-            target = out if out.ndim == 2 else out.at[index // 2]
-            target[top : top + rows_s] = grad_s[at_s]
-            target[top + rows_s : top + rows_s + rows_t] = grad_t[at_t]
-
-        for z in range(4):
-            fill(own, z, mine, z)
-            fill(send_full, z, lax.rem(mine + 4 - way, 4), z)
-            fill(keep_full, z, lax.rem(mine + 4 + way, 4), z)
+        half = 16 * rows
+        own[...] = by_x[mine].reshape(own.shape)
+        send_full[...] = by_x[lax.rem(mine + 4 - way, 4)].reshape(own.shape)
+        keep_full[...] = by_x[lax.rem(mine + 4 + way, 4)].reshape(own.shape)
         opposite = lax.rem(mine + 2, 4)
-        for z in range(2):
-            fill(send_half, z, opposite, 2 * (1 - core) + z)
-            fill(keep_half, z, opposite, 2 * core + z)
+        send_half[...] = by_x[opposite, pl.ds(pl.multiple_of((1 - core) * half, half), half)]
+        keep_half[...] = by_x[opposite, pl.ds(pl.multiple_of(core * half, half), half)]
 
 
 def backward_kernel(at, grad_pre, inner, outer, video, cot, w_rev, _, grad_video, shifts):
@@ -398,9 +382,7 @@
 
 def residual_block(video, spatial_weight, temporal_weight, cotangent):
     _, n_frames, n_rows, n_cols, chans = video.shape
-    z, x, core = (lax.axis_index(axis) for axis in ("z", "x", "core"))
-    y = lax.axis_index("y_hi") * 2 + lax.axis_index("y_lo")
-    at = (y, z, x, core)
+    x, core = lax.axis_index("x"), lax.axis_index("core")
     video, cot = video[0], cotangent[0]
     shape = (n_frames, n_rows, n_cols, chans)
     wide = (n_frames, n_rows + 2, n_cols, 3 * chans)
@@ -411,12 +393,12 @@
     rows_s, rows_t = spatial_weight.shape[0], temporal_weight.shape[0]
     rows = 8 * (rows_s + rows_t)
     last = n_frames - 1
-    at_part = [jnp.stack([y, core, base, last]).astype(jnp.int32) for base in (0, count)]
+    at_part = [jnp.stack([x, core, base, last]).astype(jnp.int32) for base in (0, count)]
     same = lambda f, base: f + base
 
     ahead = along_frames(cot[:2], -1)
     inner, outer = edge_rows(video, core)
-    units = both_kernels(spatial_weight, temporal_weight, at)
+    units = both_kernels(spatial_weight, temporal_weight, (x, core))
     shifts = None
     for part in range(2):
         shifts = part_of(
@@ -462,9 +444,9 @@
         [whole(shape_) for shape_ in block_shapes],
         [jax.ShapeDtypeStruct(shape_, F32) for shape_ in block_shapes],
         12 * pair,
-        [pltpu.VMEM(full_s, F32), pltpu.VMEM(full_t, F32)],
+        [pltpu.VMEM(full_s, F32), pltpu.VMEM(full_t, F32), pltpu.VMEM((4, 4 * rows, chans), F32)],
         scalars=1,
-        limit=28,
+        limit=32,
     )(at_part[0], shifts, grad_pre, hidden, cot, cot, cot, ahead, ahead)
     grad_video = part_of(
         backward_kernel,
@@ -493,7 +475,7 @@
         (at_part[0], video, past, past, hidden, hidden, hidden, w_t),
         3 * pair,
     )
-    spatial_part, temporal_part = summed_kernels(blocks, rows_s, rows_t, at)
+    spatial_part, temporal_part = summed_kernels(blocks, rows_s, rows_t, core)
     total_cells = n_frames * n_rows * n_cols * lax.axis_size(AXES)
     factor = float(total_cells) ** (-0.5)
     return (output[None], grad_video[None], spatial_part * factor, temporal_part * factor)

time: 149 us -> 141 us (0.946)
  the two profiles are of different devices: /device:TPU:16 before, /device:TPU:17 now
where the time goes in v2:
time: 141 us; the launch traced here: 140 us
  starting transfers between devices  46.1 us (33%)
  Pallas kernels  39.4 us (28%)
  waiting for transfers between devices  35.9 us (25%)
  local copies, waits for them, and re-layouts  13.3 us (9%)
  other arithmetic  4.25 us (3%)
    ppermute x12, starting transfers between devices, moved(): return lax.ppermute(value, AXES, ring(axis))  18.5 us
    pallas_call x4, Pallas kernels, part_of(): call(body, count, in_specs, frame_spec(out.shape, lambda f: f + base), ou...  17.8 us
    ppermute x12, waiting for transfers between devices, moved(): return lax.ppermute(value, AXES, ring(axis))  15 us
    ppermute x2, waiting for transfers between devices, along_frames(): return lax.ppermute(value, FRAME_AXES, pairs)  14.9 us
    pallas_call x1, Pallas kernels, residual_block(): call(weights_kernel, n_frames, [frame_spec(wide), frame_spec(shape), fram...  10.3 us
    pallas_call x1, Pallas kernels, residual_block(): call(forward_kernel, n_frames, [frame_spec(wide)] + cot_specs(0) + [whole...  10.3 us
    all_to_all x1, starting transfers between devices, summed_kernels(): lax.all_to_all(total, UNIT_AXES, split_axis=0, concat_axis=0, tiled=True)  9.09 us
    all_to_all x1, starting transfers between devices, both_kernels(): lax.all_to_all(copies, UNIT_AXES, split_axis=0, concat_axis=0, tiled=True)  7.74 us
  transfers between devices with their start and end apart: 18, of which 9 were waited for; matrix products, arithmetic and copies ran while one was open for 5% of the time, Pallas kernels for 13%

profile of v2, /device:TPU:17, one launch (start us, length us, event | category | flops | bytes accessed | tf_op | source)
XLA Modules:
  0.0 140.0 jit_solution(8865739994458522962)
XLA Ops:
  2.1 7.7 %all-to-all-start = ((bf16[16,24,256]{2,1,0:T(8,128)(2,1)}), bf16[16,24,256]{2,1,0:T(8,128)(2,1)S(1)}, u32[]{:S(2)}, u32[]{:S(2)}) async-start(bf16[16,24,256]{2,1,0:T(8,128)(2,1)} %broadcast_in_dim.41), calls=%async_computation | async-start | bytes 393216 | tf_op jit(solution)/shard_map/all_to_all | solution.py:85
  9.8 5.5 %all-to-all-done = bf16[16,24,256]{2,1,0:T(8,128)(2,1)S(1)} async-done(((bf16[16,24,256]{2,1,0:T(8,128)(2,1)}), bf16[16,24,256]{2,1,0:T(8,128)(2,1)S(1)}, u32[]{:S(2)}, u32[]{:S(2)}) %all-to-all-start) | async-done | bytes 196640 | tf_op jit(solution)/shard_map/all_to_all | solution.py:85
  15.3 1.8 %collective-permute-start.3 = (bf16[384,256]{1,0:T(8,128)(2,1)S(1)}, bf16[384,256]{1,0:T(8,128)(2,1)S(1)}, u32[]{:S(2)}, u32[]{:S(2)}) collective-permute-start(bf16[384,256]{1,0:T(8,128)(2,1)S(1)} %bitcast.51), channel_id=1, source_target_pairs={{0,1},{1,0},{2,3},{3,2},{4,5},{5,4},{6,7},{7,6},{8,9},{9,8},{10,11... | collective-permute-start | bytes 589832 | tf_op jit(solution)/shard_map/ppermute | solution.py:45
  17.1 1.9 %dynamic-slice_bitcast_fusion.1 = (bf16[4,1,128,256]{3,2,1,0:T(8,128)(2,1)}, bf16[4,1,128,256]{3,2,1,0:T(8,128)(2,1)}) fusion(bf16[1,4,8,128,256]{4,3,2,1,0:T(8,128)(2,1)} %param.5, s32[]{:T(128)S(6)} %select_n.54, s32[]{:T(128)S(6)} %select_n.53), kind=kLoop, calls=%fused_computation.8 | loop fusion | bytes 1048584 | tf_op jit(solution)/shard_map/dynamic_slice | solution.py:121
  19.0 3.5 %collective-permute-start.1 = (bf16[4,1,128,256]{3,2,1,0:T(8,128)(2,1)}, bf16[4,1,128,256]{3,2,1,0:T(8,128)(2,1)S(1)}, u32[]{:S(2)}, u32[]{:S(2)}) collective-permute-start(bf16[4,1,128,256]{3,2,1,0:T(8,128)(2,1)} %get-tuple-element.28), channel_id=1, source_target_pairs={{1,2},{2,1},{3,4},{4,3},{5,6},{6,5},{7,8},{8,7},{9,10},{10,9},{11,... | collective-permute-start | bytes 786440 | tf_op jit(solution)/shard_map/ppermute | solution.py:114
  22.6 2.4 %collective-permute-start.4 = (bf16[2,384,256]{2,1,0:T(8,128)(2,1)S(1)}, bf16[2,384,256]{2,1,0:T(8,128)(2,1)S(1)}, u32[]{:S(2)}, u32[]{:S(2)}) collective-permute-start(bf16[2,384,256]{2,1,0:T(8,128)(2,1)S(1)} %bitcast_dynamic-update-slice_fusion.5), channel_id=1, source_target_pairs={{0,2},{1,7},{2,4},{3,1},{4,6},{5,3},{6,0},{7,5},{8,10},{9,15},{10,... | collective-permute-start | bytes 1179656 | tf_op jit(solution)/shard_map/ppermute | solution.py:45
  25.0 2.3 %slice_bitcast_fusion = bf16[2,8,128,256]{3,2,1,0:T(8,128)(2,1)} fusion(bf16[1,4,8,128,256]{4,3,2,1,0:T(8,128)(2,1)} %param.8), kind=kLoop, calls=%fused_computation | loop fusion | bytes 2097152 | tf_op jit(solution)/shard_map/slice | solution.py:399
  27.3 3.5 %collective-permute-start.2 = (bf16[2,8,128,256]{3,2,1,0:T(8,128)(2,1)}, bf16[2,8,128,256]{3,2,1,0:T(8,128)(2,1)}, u32[]{:S(2)}, u32[]{:S(2)}) collective-permute-start(bf16[2,8,128,256]{3,2,1,0:T(8,128)(2,1)} %slice_bitcast_fusion), channel_id=1, source_target_pairs={{16,0},{32,16},{48,32},{64,48},{80,64},{96,80},{112,96},{17,1},{33... | collective-permute-start | bytes 3145736 | tf_op jit(solution)/shard_map/ppermute | solution.py:128
  30.9 2.2 %shard_map.84._ = bf16[4,10,128,768]{3,2,1,0:T(8,128)(2,1)S(1)} custom-call(s32[4]{0:T(128)S(1)} %get-tuple-element.31.at, bf16[4,8,128,256]{3,2,1,0:T(8,128)(2,1)S(1)} %bitcast.36, bf16[4,1,128,256]{3,2,1,0:T(8,128)(2,1)S(1)} %collective-permute-done.inner, bf16[4,1,128,256]{3,2,1,0:T(8,128)(2,1)S(1)} %collective-permute-done.1.outer, s32[1]{0:T(128)} %constant.56.clone.1._), custom_call_target="tpu_custom_call" | custom-call | flops 268435456 | bytes 8388608 | tf_op jit(solution)/shard_map/pallas_call | solution.py:359
  33.1 2.2 %shard_map.85.shifts = bf16[4,10,128,768]{3,2,1,0:T(8,128)(2,1)S(1)} custom-call(s32[4]{0:T(128)S(1)} %get-tuple-element.30.at, bf16[4,8,128,256]{3,2,1,0:T(8,128)(2,1)S(1)} %bitcast.37, bf16[4,1,128,256]{3,2,1,0:T(8,128)(2,1)S(1)} %collective-permute-done.inner, ...), custom_call_target="tpu_custom_call", output_to_operand_aliasing={{}: (4, {})} | custom-call | flops 268435456 | bytes 8388608 | tf_op jit(solution)/shard_map/pallas_call | solution.py:359
  35.6 3.4 %collective-permute-start.6 = (bf16[384,256]{1,0:T(8,128)(2,1)S(1)}, bf16[384,256]{1,0:T(8,128)(2,1)S(1)}, u32[]{:S(2)}, u32[]{:S(2)}) collective-permute-start(bf16[384,256]{1,0:T(8,128)(2,1)S(1)} %dynamic-slice_bitcast_fusion.3), channel_id=1, source_target_pairs={{0,2},{1,7},{2,4},{3,1},{4,6},{5,3},{6,0},{7,5},{8,10},{9,15},{10,... | collective-permute-start | bytes 589832 | tf_op jit(solution)/shard_map/ppermute | solution.py:45
  39.1 2.6 %collective-permute-done.6 = bf16[384,256]{1,0:T(8,128)(2,1)S(1)} collective-permute-done((bf16[384,256]{1,0:T(8,128)(2,1)S(1)}, bf16[384,256]{1,0:T(8,128)(2,1)S(1)}, u32[]{:S(2)}, u32[]{:S(2)}) %collective-permute-start.6) | collective-permute-done | bytes 196640 | tf_op jit(solution)/shard_map/ppermute | solution.py:45
  41.7 1.8 %collective-permute-start.7 = (bf16[384,256]{1,0:T(8,128)(2,1)S(1)}, bf16[384,256]{1,0:T(8,128)(2,1)S(1)}, u32[]{:S(2)}, u32[]{:S(2)}) collective-permute-start(bf16[384,256]{1,0:T(8,128)(2,1)S(1)} %collective-permute-done.6), channel_id=1, source_target_pairs={{0,1},{1,0},{2,3},{3,2},{4,5},{5,4},{6,7},{7,6},{8,9},{9,8},{10,11... | collective-permute-start | bytes 589832 | tf_op jit(solution)/shard_map/ppermute | solution.py:45
  45.2 8.6 %collective-permute-done.2.ahead1.ahead2 = bf16[2,8,128,256]{3,2,1,0:T(8,128)(2,1)} collective-permute-done((bf16[2,8,128,256]{3,2,1,0:T(8,128)(2,1)}, bf16[2,8,128,256]{3,2,1,0:T(8,128)(2,1)}, u32[]{:S(2)}, u32[]{:S(2)}) %collective-permute-start.2) | collective-permute-done | bytes 1048608 | tf_op jit(solution)/shard_map/ppermute | solution.py:128
  53.8 10.3 %shard_map.87 = (bf16[4,8,128,256]{3,2,1,0:T(8,128)(2,1)S(1)}, bf16[4,8,128,256]{3,2,1,0:T(8,128)(2,1)S(1)}, bf16[4,1,128,256]{3,2,1,0:T(8,128)(2,1)}, bf16[4,1,128,256]{3,2,1,0:T(8,128)(2,1)}) custom-call(s32[4]{0:T(128)S(1)} %get-tuple-element.31.at, bf16[4,10,128,768]{3,2,1,0:T(8,128)(2,1)S(1)} %shard_map.85.shifts, ...), custom_call_target="tpu_custom_call" | custom-call | flops 6442450944 | bytes 8388608 | tf_op jit(solution)/shard_map/pallas_call | solution.py:427
  64.1 10.3 %shard_map.91 = (f32[2,384,256]{2,1,0:T(8,128)S(1)}, f32[384,256]{1,0:T(8,128)S(1)}, f32[384,256]{1,0:T(8,128)S(1)}, f32[2,384,256]{2,1,0:T(8,128)S(1)}, f32[2,384,256]{2,1,0:T(8,128)S(1)}) custom-call(s32[4]{0:T(128)S(1)} %get-tuple-element.31.at, bf16[4,10,128,768]{3,2,1,0:T(8,128)(2,1)S(1)} %shard_map.85.shifts, ...), custom_call_target="tpu_custom_call" | custom-call | flops 6442450944 | bytes 8388608 | tf_op jit(solution)/shard_map/pallas_call | solution.py:440
  75.0 1.2 collective-permute-done.12
  76.3 1.5 %collective-permute-start.13 = (f32[384,256]{1,0:T(8,128)S(1)}, f32[384,256]{1,0:T(8,128)S(1)}, u32[]{:S(2)}, u32[]{:S(2)}) collective-permute-start(f32[384,256]{1,0:T(8,128)S(1)} %add.80), channel_id=1, source_target_pairs={{0,2},{1,7},{2,4},{3,1},{4,6},{5,3},{6,0},{7,5},{8,10},{9,15},{10,... | collective-permute-start | bytes 1179656 | tf_op jit(solution)/shard_map/ppermute | solution.py:45
  77.8 5.5 %collective-permute-done.13 = f32[384,256]{1,0:T(8,128)S(1)} collective-permute-done((f32[384,256]{1,0:T(8,128)S(1)}, f32[384,256]{1,0:T(8,128)S(1)}, u32[]{:S(2)}, u32[]{:S(2)}) %collective-permute-start.13) | collective-permute-done | bytes 393248 | tf_op jit(solution)/shard_map/ppermute | solution.py:45
  83.5 2.4 %collective-permute-start.14 = (bf16[2,384,256]{2,1,0:T(8,128)(2,1)S(1)}, bf16[2,384,256]{2,1,0:T(8,128)(2,1)S(1)}, u32[]{:S(2)}, u32[]{:S(2)}) collective-permute-start(bf16[2,384,256]{2,1,0:T(8,128)(2,1)S(1)} %add_convert_fusion), channel_id=1, source_target_pairs={{0,2},{1,7},{2,4},{3,1},{4,6},{5,3},{6,0},{7,5},{8,10},{9,15},{10,... | collective-permute-start | bytes 1179656 | tf_op jit(solution)/shard_map/ppermute | solution.py:45
  85.9 4.7 %collective-permute-done.14 = bf16[2,384,256]{2,1,0:T(8,128)(2,1)S(1)} collective-permute-done((bf16[2,384,256]{2,1,0:T(8,128)(2,1)S(1)}, bf16[2,384,256]{2,1,0:T(8,128)(2,1)S(1)}, u32[]{:S(2)}, u32[]{:S(2)}) %collective-permute-start.14) | collective-permute-done | bytes 393248 | tf_op jit(solution)/shard_map/ppermute | solution.py:45
  90.8 4.2 %collective-permute-start.15 = (f32[16,24,256]{2,1,0:T(8,128)S(1)}, f32[16,24,256]{2,1,0:T(8,128)S(1)}, u32[]{:S(2)}, u32[]{:S(2)}) collective-permute-start(f32[16,24,256]{2,1,0:T(8,128)S(1)} %dynamic-slice_bitcast_fusion), channel_id=1, source_target_pairs={{0,1},{1,0},{2,3},{3,2},{4,5},{5,4},{6,7},{7,6},{8,9},{9,8},{10,11... | collective-permute-start | bytes 1179656 | tf_op jit(solution)/shard_map/ppermute | solution.py:45
  96.1 1.9 %collective-permute-start.8 = (bf16[2,8,128,256]{3,2,1,0:T(8,128)(2,1)}, bf16[2,8,128,256]{3,2,1,0:T(8,128)(2,1)S(1)}, u32[]{:S(2)}, u32[]{:S(2)}) collective-permute-start(bf16[2,8,128,256]{3,2,1,0:T(8,128)(2,1)} %slice.17), channel_id=1, source_target_pairs={{0,16},{16,32},{32,48},{48,64},{64,80},{80,96},{96,112},{1,17},{17... | collective-permute-start | bytes 3145736 | tf_op jit(solution)/shard_map/ppermute | solution.py:128
  98.0 1.9 %collective-permute-start.10 = (bf16[4,1,128,256]{3,2,1,0:T(8,128)(2,1)}, bf16[4,1,128,256]{3,2,1,0:T(8,128)(2,1)}, u32[]{:S(2)}, u32[]{:S(2)}) collective-permute-start(bf16[4,1,128,256]{3,2,1,0:T(8,128)(2,1)} %get-tuple-element.22), channel_id=1, source_target_pairs={{1,2},{2,1},{3,4},{4,3},{5,6},{6,5},{7,8},{8,7},{9,10},{10,9},{11,... | collective-permute-start | bytes 786440 | tf_op jit(solution)/shard_map/ppermute | solution.py:114
  102.4 9.1 %all-to-all-start.1 = ((f32[16,24,256]{2,1,0:T(8,128)}), f32[16,24,256]{2,1,0:T(8,128)}, u32[]{:S(2)}, u32[]{:S(2)}) async-start(f32[16,24,256]{2,1,0:T(8,128)} %bitcast_add_fusion), calls=%async_computation.1 | async-start | bytes 786432 | tf_op jit(solution)/shard_map/all_to_all | solution.py:105
  111.5 1.6 %copy-done.1 = bf16[1,4,8,128,256]{4,3,2,1,0:T(8,128)(2,1)S(1)} copy-done((bf16[1,4,8,128,256]{4,3,2,1,0:T(8,128)(2,1)S(1)}, bf16[1,4,8,128,256]{4,3,2,1,0:T(8,128)(2,1)}, u32[]{:S(2)}) %copy-start.1) | copy-done | bytes 2097176
  113.1 1.3 copy-done.3
  114.4 1.6 %copy-done.5 = bf16[1,4,8,128,256]{4,3,2,1,0:T(8,128)(2,1)S(1)} copy-done((bf16[1,4,8,128,256]{4,3,2,1,0:T(8,128)(2,1)S(1)}, bf16[1,4,8,128,256]{4,3,2,1,0:T(8,128)(2,1)}, u32[]{:S(2)}) %copy-start.5) | copy-done | bytes 2097176
  116.0 1.6 %copy-done.8 = bf16[4,8,128,256]{3,2,1,0:T(8,128)(2,1)S(1)} copy-done((bf16[4,8,128,256]{3,2,1,0:T(8,128)(2,1)S(1)}, bf16[4,8,128,256]{3,2,1,0:T(8,128)(2,1)}, u32[]{:S(2)}) %copy-start.8) | copy-done | bytes 2097176
  117.6 9.6 %shard_map.90 = bf16[4,8,128,256]{3,2,1,0:T(8,128)(2,1)} custom-call(s32[4]{0:T(128)S(1)} %get-tuple-element.31.at, bf16[4,8,128,256]{3,2,1,0:T(8,128)(2,1)S(1)} %copy-done.8, bf16[4,1,128,256]{3,2,1,0:T(8,128)(2,1)} %collective-permute-done.9.inner, bf16[4,1,128,256]{3,2,1,0:T(8,128)(2,1)} %collective-permute-done.10.outer, ...), custom_call_target="tpu_custom_call" | custom-call | flops 4831838208 | bytes 8388608 | tf_op jit(solution)/shard_map/pallas_call | solution.py:359
  127.2 6.3 %collective-permute-done.8.past0.past1 = bf16[2,8,128,256]{3,2,1,0:T(8,128)(2,1)S(1)} collective-permute-done((bf16[2,8,128,256]{3,2,1,0:T(8,128)(2,1)}, bf16[2,8,128,256]{3,2,1,0:T(8,128)(2,1)S(1)}, u32[]{:S(2)}, u32[]{:S(2)}) %collective-permute-start.8) | collective-permute-done | bytes 1048608 | tf_op jit(solution)/shard_map/ppermute | solution.py:128
  133.4 3.9 %shard_map.88 = bf16[4,8,128,256]{3,2,1,0:T(8,128)(2,1)} custom-call(s32[4]{0:T(128)S(1)} %get-tuple-element.31.at, bf16[4,8,128,256]{3,2,1,0:T(8,128)(2,1)S(1)} %bitcast.39, bf16[2,8,128,256]{3,2,1,0:T(8,128)(2,1)S(1)} %collective-permute-done.8.past0.past1, bf16[2,8,128,256]{3,2,1,0:T(8,128)(2,1)S(1)} %collective-permute-done.8.past0.past1, ...), custom_call_target="tpu_custom_call" | custom-call | flops 1610612736 | bytes 8388608 | tf_op jit(solution)/shard_map/pallas_call | solution.py:359
  (55 shorter events, 10.8 us)
Async XLA Ops:
  2.1 13.3 %all-to-all-start = ((bf16[16,24,256]{2,1,0:T(8,128)(2,1)}), bf16[16,24,256]{2,1,0:T(8,128)(2,1)S(1)}, u32[]{:S(2)}, u32[]{:S(2)}) async-start(bf16[16,24,256]{2,1,0:T(8,128)(2,1)} %broadcast_in_dim.41), calls=%async_computation | async-start | bytes 393216 | tf_op jit(solution)/shard_map/all_to_all | solution.py:85
  15.3 7.3 %collective-permute-start.3 = (bf16[384,256]{1,0:T(8,128)(2,1)S(1)}, bf16[384,256]{1,0:T(8,128)(2,1)S(1)}, u32[]{:S(2)}, u32[]{:S(2)}) collective-permute-start(bf16[384,256]{1,0:T(8,128)(2,1)S(1)} %bitcast.51), channel_id=1, source_target_pairs={{0,1},{1,0},{2,3},{3,2},{4,5},{5,4},{6,7},{7,6},{8,9},{9,8},{10,11... | collective-permute-start | bytes 589832 | tf_op jit(solution)/shard_map/ppermute | solution.py:45
  19.0 11.9 %collective-permute-start = (bf16[4,1,128,256]{3,2,1,0:T(8,128)(2,1)}, bf16[4,1,128,256]{3,2,1,0:T(8,128)(2,1)S(1)}, u32[]{:S(2)}, u32[]{:S(2)}) collective-permute-start(bf16[4,1,128,256]{3,2,1,0:T(8,128)(2,1)} %get-tuple-element.29), channel_id=1, source_target_pairs={{0,1},{1,0},{2,3},{3,2},{4,5},{5,4},{6,7},{7,6},{8,9},{9,8},{10,11... | collective-permute-start | bytes 786440 | tf_op jit(solution)/shard_map/ppermute | solution.py:45
  19.0 11.9 %collective-permute-start.1 = (bf16[4,1,128,256]{3,2,1,0:T(8,128)(2,1)}, bf16[4,1,128,256]{3,2,1,0:T(8,128)(2,1)S(1)}, u32[]{:S(2)}, u32[]{:S(2)}) collective-permute-start(bf16[4,1,128,256]{3,2,1,0:T(8,128)(2,1)} %get-tuple-element.28), channel_id=1, source_target_pairs={{1,2},{2,1},{3,4},{4,3},{5,6},{6,5},{7,8},{8,7},{9,10},{10,9},{11,... | collective-permute-start | bytes 786440 | tf_op jit(solution)/shard_map/ppermute | solution.py:114
  22.5 8.4 %copy-start = (bf16[1,4,8,128,256]{4,3,2,1,0:T(8,128)(2,1)S(1)}, bf16[1,4,8,128,256]{4,3,2,1,0:T(8,128)(2,1)}, u32[]{:S(2)}) copy-start(bf16[1,4,8,128,256]{4,3,2,1,0:T(8,128)(2,1)} %param.5) | copy-start | bytes 6291460
  22.6 12.7 %collective-permute-start.4 = (bf16[2,384,256]{2,1,0:T(8,128)(2,1)S(1)}, bf16[2,384,256]{2,1,0:T(8,128)(2,1)S(1)}, u32[]{:S(2)}, u32[]{:S(2)}) collective-permute-start(bf16[2,384,256]{2,1,0:T(8,128)(2,1)S(1)} %bitcast_dynamic-update-slice_fusion.5), channel_id=1, source_target_pairs={{0,2},{1,7},{2,4},{3,1},{4,6},{5,3},{6,0},{7,5},{8,10},{9,15},{10,... | collective-permute-start | bytes 1179656 | tf_op jit(solution)/shard_map/ppermute | solution.py:45
  27.3 26.5 %collective-permute-start.2 = (bf16[2,8,128,256]{3,2,1,0:T(8,128)(2,1)}, bf16[2,8,128,256]{3,2,1,0:T(8,128)(2,1)}, u32[]{:S(2)}, u32[]{:S(2)}) collective-permute-start(bf16[2,8,128,256]{3,2,1,0:T(8,128)(2,1)} %slice_bitcast_fusion), channel_id=1, source_target_pairs={{16,0},{32,16},{48,32},{64,48},{80,64},{96,80},{112,96},{17,1},{33... | collective-permute-start | bytes 3145736 | tf_op jit(solution)/shard_map/ppermute | solution.py:128
  35.3 8.2 %collective-permute-start.5 = (bf16[2,384,256]{2,1,0:T(8,128)(2,1)S(1)}, bf16[2,384,256]{2,1,0:T(8,128)(2,1)S(1)}, u32[]{:S(2)}, u32[]{:S(2)}) collective-permute-start(bf16[2,384,256]{2,1,0:T(8,128)(2,1)S(1)} %collective-permute-done.4), channel_id=1, source_target_pairs={{0,1},{1,0},{2,3},{3,2},{4,5},{5,4},{6,7},{7,6},{8,9},{9,8},{10,11... | collective-permute-start | bytes 1179656 | tf_op jit(solution)/shard_map/ppermute | solution.py:45
  35.6 9.0 %copy-start.6 = (bf16[192,192]{1,0:T(8,128)(2,1)S(1)}, bf16[192,192]{1,0:T(8,128)(2,1)}, u32[]{:S(2)}) copy-start(bf16[192,192]{1,0:T(8,128)(2,1)} %constant.69.clone.order) | copy-start | bytes 221188
  35.6 6.1 %collective-permute-start.6 = (bf16[384,256]{1,0:T(8,128)(2,1)S(1)}, bf16[384,256]{1,0:T(8,128)(2,1)S(1)}, u32[]{:S(2)}, u32[]{:S(2)}) collective-permute-start(bf16[384,256]{1,0:T(8,128)(2,1)S(1)} %dynamic-slice_bitcast_fusion.3), channel_id=1, source_target_pairs={{0,2},{1,7},{2,4},{3,1},{4,6},{5,3},{6,0},{7,5},{8,10},{9,15},{10,... | collective-permute-start | bytes 589832 | tf_op jit(solution)/shard_map/ppermute | solution.py:45
  39.1 14.7 %copy-start.4 = (bf16[1,4,8,128,256]{4,3,2,1,0:T(8,128)(2,1)S(1)}, bf16[1,4,8,128,256]{4,3,2,1,0:T(8,128)(2,1)}, u32[]{:S(2)}) copy-start(bf16[1,4,8,128,256]{4,3,2,1,0:T(8,128)(2,1)} %param.8) | copy-start | bytes 6291460
  41.7 2.9 %collective-permute-start.7 = (bf16[384,256]{1,0:T(8,128)(2,1)S(1)}, bf16[384,256]{1,0:T(8,128)(2,1)S(1)}, u32[]{:S(2)}, u32[]{:S(2)}) collective-permute-start(bf16[384,256]{1,0:T(8,128)(2,1)S(1)} %collective-permute-done.6), channel_id=1, source_target_pairs={{0,1},{1,0},{2,3},{3,2},{4,5},{5,4},{6,7},{7,6},{8,9},{9,8},{10,11... | collective-permute-start | bytes 589832 | tf_op jit(solution)/shard_map/ppermute | solution.py:45
  64.1 10.3 %copy-start.7 = (bf16[4,8,128,256]{3,2,1,0:T(8,128)(2,1)}, bf16[4,8,128,256]{3,2,1,0:T(8,128)(2,1)S(1)}, u32[]{:S(2)}) copy-start(bf16[4,8,128,256]{3,2,1,0:T(8,128)(2,1)S(1)} %get-tuple-element.20.grad_pre) | copy-start | bytes 6291460
  74.4 1.8 %collective-permute-start.12 = (f32[384,256]{1,0:T(8,128)S(1)}, f32[384,256]{1,0:T(8,128)S(1)}, u32[]{:S(2)}, u32[]{:S(2)}) collective-permute-start(f32[384,256]{1,0:T(8,128)S(1)} %get-tuple-element.27), channel_id=1, source_target_pairs={{0,1},{1,0},{2,3},{3,2},{4,5},{5,4},{6,7},{7,6},{8,9},{9,8},{10,11... | collective-permute-start | bytes 1179656 | tf_op jit(solution)/shard_map/ppermute | solution.py:45
  74.7 8.6 %collective-permute-start.11 = (f32[2,384,256]{2,1,0:T(8,128)S(1)}, f32[2,384,256]{2,1,0:T(8,128)S(1)}, u32[]{:S(2)}, u32[]{:S(2)}) collective-permute-start(f32[2,384,256]{2,1,0:T(8,128)S(1)} %get-tuple-element.25), channel_id=1, source_target_pairs={{0,1},{1,0},{2,3},{3,2},{4,5},{5,4},{6,7},{7,6},{8,9},{9,8},{10,11... | collective-permute-start | bytes 2359304 | tf_op jit(solution)/shard_map/ppermute | solution.py:45
  76.3 7.0 %collective-permute-start.13 = (f32[384,256]{1,0:T(8,128)S(1)}, f32[384,256]{1,0:T(8,128)S(1)}, u32[]{:S(2)}, u32[]{:S(2)}) collective-permute-start(f32[384,256]{1,0:T(8,128)S(1)} %add.80), channel_id=1, source_target_pairs={{0,2},{1,7},{2,4},{3,1},{4,6},{5,3},{6,0},{7,5},{8,10},{9,15},{10,... | collective-permute-start | bytes 1179656 | tf_op jit(solution)/shard_map/ppermute | solution.py:45
  83.5 7.1 %collective-permute-start.14 = (bf16[2,384,256]{2,1,0:T(8,128)(2,1)S(1)}, bf16[2,384,256]{2,1,0:T(8,128)(2,1)S(1)}, u32[]{:S(2)}, u32[]{:S(2)}) collective-permute-start(bf16[2,384,256]{2,1,0:T(8,128)(2,1)S(1)} %add_convert_fusion), channel_id=1, source_target_pairs={{0,2},{1,7},{2,4},{3,1},{4,6},{5,3},{6,0},{7,5},{8,10},{9,15},{10,... | collective-permute-start | bytes 1179656 | tf_op jit(solution)/shard_map/ppermute | solution.py:45
  90.8 10.8 %collective-permute-start.15 = (f32[16,24,256]{2,1,0:T(8,128)S(1)}, f32[16,24,256]{2,1,0:T(8,128)S(1)}, u32[]{:S(2)}, u32[]{:S(2)}) collective-permute-start(f32[16,24,256]{2,1,0:T(8,128)S(1)} %dynamic-slice_bitcast_fusion), channel_id=1, source_target_pairs={{0,1},{1,0},{2,3},{3,2},{4,5},{5,4},{6,7},{7,6},{8,9},{9,8},{10,11... | collective-permute-start | bytes 1179656 | tf_op jit(solution)/shard_map/ppermute | solution.py:45
  96.1 37.4 %collective-permute-start.8 = (bf16[2,8,128,256]{3,2,1,0:T(8,128)(2,1)}, bf16[2,8,128,256]{3,2,1,0:T(8,128)(2,1)S(1)}, u32[]{:S(2)}, u32[]{:S(2)}) collective-permute-start(bf16[2,8,128,256]{3,2,1,0:T(8,128)(2,1)} %slice.17), channel_id=1, source_target_pairs={{0,16},{16,32},{32,48},{48,64},{64,80},{80,96},{96,112},{1,17},{17... | collective-permute-start | bytes 3145736 | tf_op jit(solution)/shard_map/ppermute | solution.py:128
  98.0 13.5 %collective-permute-start.10 = (bf16[4,1,128,256]{3,2,1,0:T(8,128)(2,1)}, bf16[4,1,128,256]{3,2,1,0:T(8,128)(2,1)}, u32[]{:S(2)}, u32[]{:S(2)}) collective-permute-start(bf16[4,1,128,256]{3,2,1,0:T(8,128)(2,1)} %get-tuple-element.22), channel_id=1, source_target_pairs={{1,2},{2,1},{3,4},{4,3},{5,6},{6,5},{7,8},{8,7},{9,10},{10,9},{11,... | collective-permute-start | bytes 786440 | tf_op jit(solution)/shard_map/ppermute | solution.py:114
  99.9 11.6 %collective-permute-start.9 = (bf16[4,1,128,256]{3,2,1,0:T(8,128)(2,1)}, bf16[4,1,128,256]{3,2,1,0:T(8,128)(2,1)}, u32[]{:S(2)}, u32[]{:S(2)}) collective-permute-start(bf16[4,1,128,256]{3,2,1,0:T(8,128)(2,1)} %get-tuple-element.21), channel_id=1, source_target_pairs={{0,1},{1,0},{2,3},{3,2},{4,5},{5,4},{6,7},{7,6},{8,9},{9,8},{10,11... | collective-permute-start | bytes 786440 | tf_op jit(solution)/shard_map/ppermute | solution.py:45
  100.5 1.0 copy-start.2
  102.4 35.4 %all-to-all-start.1 = ((f32[16,24,256]{2,1,0:T(8,128)}), f32[16,24,256]{2,1,0:T(8,128)}, u32[]{:S(2)}, u32[]{:S(2)}) async-start(f32[16,24,256]{2,1,0:T(8,128)} %bitcast_add_fusion), calls=%async_computation.1 | async-start | bytes 786432 | tf_op jit(solution)/shard_map/all_to_all | solution.py:105
  111.5 1.6 %copy-start.1 = (bf16[1,4,8,128,256]{4,3,2,1,0:T(8,128)(2,1)S(1)}, bf16[1,4,8,128,256]{4,3,2,1,0:T(8,128)(2,1)}, u32[]{:S(2)}) copy-start(bf16[1,4,8,128,256]{4,3,2,1,0:T(8,128)(2,1)} %param.5) | copy-start | bytes 6291460
  113.1 1.3 copy-start.3
  114.4 1.6 %copy-start.5 = (bf16[1,4,8,128,256]{4,3,2,1,0:T(8,128)(2,1)S(1)}, bf16[1,4,8,128,256]{4,3,2,1,0:T(8,128)(2,1)}, u32[]{:S(2)}) copy-start(bf16[1,4,8,128,256]{4,3,2,1,0:T(8,128)(2,1)} %param.8) | copy-start | bytes 6291460
  116.0 1.6 %copy-start.8 = (bf16[4,8,128,256]{3,2,1,0:T(8,128)(2,1)S(1)}, bf16[4,8,128,256]{3,2,1,0:T(8,128)(2,1)}, u32[]{:S(2)}) copy-start(bf16[4,8,128,256]{3,2,1,0:T(8,128)(2,1)} %copy-done.7) | copy-start | bytes 6291460

commit v3 on v2

--- a/solution.py
+++ b/solution.py
@@ -198,8 +198,9 @@
 
 
 def forward_kernel(
-    at, shifts, cot0, cot1, cot2, ahead1, ahead2, w_s, w_back, hidden, grad_pre, inner, outer
+    at, shifts, cot0, cot1, cot2, ahead1, ahead2, w_s, w_back, *outputs
 ):
+    hidden, grad_pre, inner, outer = outputs[-4:]
     _, n_rows, n_cols, chans = hidden.shape
     step, frame = 4, at[2] + pl.program_id(0)
     for row in range(0, n_rows, step):
@@ -323,7 +324,7 @@
 
 def call(
     body, n_frames, in_specs, out_specs, out_shape, flops, scratch=(), scalars=0, aliases={},
-    limit=20,
+    limit=16,
 ):
     return pl.pallas_call(
         body,
@@ -341,7 +342,7 @@
     )
 
 
-def part_of(body, part, parts, specs, out, args, flops, scratch=(), before=None):
+def part_of(body, part, parts, specs, out, args, flops, scratch=(), before=None, limit=12):
     count = out.shape[0] // parts
     base = part * count
     in_specs = []
@@ -366,6 +367,7 @@
         scratch,
         1,
         aliases,
+        limit,
     )(*args, before)
 
 
@@ -424,15 +426,26 @@
             frame_spec(half, lambda f, k=k: jnp.maximum(f + base + k - last - 1, 0)) for k in (1, 2)
         ]
 
-    hidden, grad_pre, edge_in, edge_out = call(
-        forward_kernel,
-        n_frames,
-        [frame_spec(wide)] + cot_specs(0) + [whole(full_s), whole(full_t)],
-        [frame_spec(shape)] * 2 + [frame_spec(edge)] * 2,
-        [jax.ShapeDtypeStruct(shape, BF16)] * 2 + [jax.ShapeDtypeStruct(edge, BF16)] * 2,
-        12 * pair,
-        scalars=1,
-    )(at_part[0], shifts, cot, cot, cot, ahead, ahead, w_s, w_back)
+    forward_shapes = (shape, shape, edge, edge)
+    results = ()
+    for part in range(2):
+        base = part * count
+        after = ahead if part else cot
+        inputs = 8 + 1
+        results = call(
+            forward_kernel,
+            count,
+            [frame_spec(wide, lambda f, base=base: f + base)]
+            + cot_specs(base)
+            + [whole(full_s), whole(full_t)]
+            + [pl.BlockSpec(memory_space=pl.ANY)] * len(results),
+            [frame_spec(out, lambda f, base=base: f + base) for out in forward_shapes],
+            [jax.ShapeDtypeStruct(out, BF16) for out in forward_shapes],
+            12 * pair,
+            scalars=1,
+            aliases={inputs + i: i for i in range(len(results))},
+        )(at_part[part], shifts, cot, cot, cot, after, after, w_s, w_back, *results)
+    hidden, grad_pre, edge_in, edge_out = results
     edges = traded_edges(edge_in, edge_out)
     past = along_frames(hidden[count:], 1)
     block, half_block = (2, 2 * rows, chans), (2 * rows, chans)
@@ -446,7 +459,7 @@
         12 * pair,
         [pltpu.VMEM(full_s, F32), pltpu.VMEM(full_t, F32), pltpu.VMEM((4, 4 * rows, chans), F32)],
         scalars=1,
-        limit=32,
+        limit=26,
     )(at_part[0], shifts, grad_pre, hidden, cot, cot, cot, ahead, ahead)
     grad_video = part_of(
         backward_kernel,

time: 141 us -> 137 us (0.972)
  waiting for transfers between devices: 35.9 us -> 30.9 us
    ppermute x2, waiting for transfers between devices: 14.9 us -> 9.87 us  [along_frames(): return lax.ppermute(value, FRAME_AXES, pairs)]
    pallas_call x1 -> x2, Pallas kernels: 10.3 us -> 11.6 us  [residual_block(): call(forward_kernel, count, [frame_spec(wide, lambda f, base=base: f + ba...]
  transfers between devices with their start and end apart: 18 -> 18, of which waited for: 9 -> 9; matrix products, arithmetic and copies ran while one was open for 5% -> 5% of each run, Pallas kernels for 13% -> 18%
where the time goes in v3:
time: 137 us; the launch traced here: 136 us
  starting transfers between devices  46.1 us (34%)
  Pallas kernels  40.8 us (30%)
  waiting for transfers between devices  30.9 us (23%)
  local copies, waits for them, and re-layouts  13.3 us (10%)
  other arithmetic  4.26 us (3%)
    ppermute x12, starting transfers between devices, moved(): return lax.ppermute(value, AXES, ring(axis))  18.5 us
    pallas_call x4, Pallas kernels, part_of(): call(body, count, in_specs, frame_spec(out.shape, lambda f: f + base), ou...  17.8 us
    ppermute x12, waiting for transfers between devices, moved(): return lax.ppermute(value, AXES, ring(axis))  15 us
    pallas_call x2, Pallas kernels, residual_block(): call(forward_kernel, count, [frame_spec(wide, lambda f, base=base: f + ba...  11.6 us
    pallas_call x1, Pallas kernels, residual_block(): call(weights_kernel, n_frames, [frame_spec(wide), frame_spec(shape), fram...  10.3 us
    ppermute x2, waiting for transfers between devices, along_frames(): return lax.ppermute(value, FRAME_AXES, pairs)  9.87 us
    all_to_all x1, starting transfers between devices, summed_kernels(): lax.all_to_all(total, UNIT_AXES, split_axis=0, concat_axis=0, tiled=True)  9.09 us
    all_to_all x1, starting transfers between devices, both_kernels(): lax.all_to_all(copies, UNIT_AXES, split_axis=0, concat_axis=0, tiled=True)  7.74 us
  transfers between devices with their start and end apart: 18, of which 9 were waited for; matrix products, arithmetic and copies ran while one was open for 5% of the time, Pallas kernels for 18%

profile of v3, /device:TPU:17, one launch (start us, length us, event | category | flops | bytes accessed | tf_op | source)
XLA Modules:
  0.0 136.4 jit_solution(6801961653908537453)
XLA Ops:
  2.1 7.7 %all-to-all-start = ((bf16[16,24,256]{2,1,0:T(8,128)(2,1)}), bf16[16,24,256]{2,1,0:T(8,128)(2,1)S(1)}, u32[]{:S(2)}, u32[]{:S(2)}) async-start(bf16[16,24,256]{2,1,0:T(8,128)(2,1)} %broadcast_in_dim.41), calls=%async_computation | async-start | bytes 393216 | tf_op jit(solution)/shard_map/all_to_all | solution.py:85
  9.8 5.5 %all-to-all-done = bf16[16,24,256]{2,1,0:T(8,128)(2,1)S(1)} async-done(((bf16[16,24,256]{2,1,0:T(8,128)(2,1)}), bf16[16,24,256]{2,1,0:T(8,128)(2,1)S(1)}, u32[]{:S(2)}, u32[]{:S(2)}) %all-to-all-start) | async-done | bytes 196640 | tf_op jit(solution)/shard_map/all_to_all | solution.py:85
  15.3 1.8 %collective-permute-start.3 = (bf16[384,256]{1,0:T(8,128)(2,1)S(1)}, bf16[384,256]{1,0:T(8,128)(2,1)S(1)}, u32[]{:S(2)}, u32[]{:S(2)}) collective-permute-start(bf16[384,256]{1,0:T(8,128)(2,1)S(1)} %bitcast.56), channel_id=1, source_target_pairs={{0,1},{1,0},{2,3},{3,2},{4,5},{5,4},{6,7},{7,6},{8,9},{9,8},{10,11... | collective-permute-start | bytes 589832 | tf_op jit(solution)/shard_map/ppermute | solution.py:45
  17.1 1.9 %dynamic-slice_bitcast_fusion.1 = (bf16[4,1,128,256]{3,2,1,0:T(8,128)(2,1)}, bf16[4,1,128,256]{3,2,1,0:T(8,128)(2,1)}) fusion(bf16[1,4,8,128,256]{4,3,2,1,0:T(8,128)(2,1)} %param.5, s32[]{:T(128)S(6)} %select_n.54, s32[]{:T(128)S(6)} %select_n.53), kind=kLoop, calls=%fused_computation.8 | loop fusion | bytes 1048584 | tf_op jit(solution)/shard_map/dynamic_slice | solution.py:121
  19.0 3.5 %collective-permute-start.1 = (bf16[4,1,128,256]{3,2,1,0:T(8,128)(2,1)}, bf16[4,1,128,256]{3,2,1,0:T(8,128)(2,1)S(1)}, u32[]{:S(2)}, u32[]{:S(2)}) collective-permute-start(bf16[4,1,128,256]{3,2,1,0:T(8,128)(2,1)} %get-tuple-element.36), channel_id=1, source_target_pairs={{1,2},{2,1},{3,4},{4,3},{5,6},{6,5},{7,8},{8,7},{9,10},{10,9},{11,... | collective-permute-start | bytes 786440 | tf_op jit(solution)/shard_map/ppermute | solution.py:114
  22.6 2.4 %collective-permute-start.4 = (bf16[2,384,256]{2,1,0:T(8,128)(2,1)S(1)}, bf16[2,384,256]{2,1,0:T(8,128)(2,1)S(1)}, u32[]{:S(2)}, u32[]{:S(2)}) collective-permute-start(bf16[2,384,256]{2,1,0:T(8,128)(2,1)S(1)} %bitcast_dynamic-update-slice_fusion.5), channel_id=1, source_target_pairs={{0,2},{1,7},{2,4},{3,1},{4,6},{5,3},{6,0},{7,5},{8,10},{9,15},{10,... | collective-permute-start | bytes 1179656 | tf_op jit(solution)/shard_map/ppermute | solution.py:45
  25.0 2.3 %slice_bitcast_fusion = bf16[2,8,128,256]{3,2,1,0:T(8,128)(2,1)} fusion(bf16[1,4,8,128,256]{4,3,2,1,0:T(8,128)(2,1)} %param.8), kind=kLoop, calls=%fused_computation | loop fusion | bytes 2097152 | tf_op jit(solution)/shard_map/slice | solution.py:401
  27.3 3.5 %collective-permute-start.2 = (bf16[2,8,128,256]{3,2,1,0:T(8,128)(2,1)}, bf16[2,8,128,256]{3,2,1,0:T(8,128)(2,1)}, u32[]{:S(2)}, u32[]{:S(2)}) collective-permute-start(bf16[2,8,128,256]{3,2,1,0:T(8,128)(2,1)} %slice_bitcast_fusion), channel_id=1, source_target_pairs={{16,0},{32,16},{48,32},{64,48},{80,64},{96,80},{112,96},{17,1},{33... | collective-permute-start | bytes 3145736 | tf_op jit(solution)/shard_map/ppermute | solution.py:128
  30.9 2.2 %shard_map.84._ = bf16[4,10,128,768]{3,2,1,0:T(8,128)(2,1)S(1)} custom-call(s32[4]{0:T(128)S(1)} %get-tuple-element.39.at, bf16[4,8,128,256]{3,2,1,0:T(8,128)(2,1)S(1)} %bitcast.36, bf16[4,1,128,256]{3,2,1,0:T(8,128)(2,1)S(1)} %collective-permute-done.inner, bf16[4,1,128,256]{3,2,1,0:T(8,128)(2,1)S(1)} %collective-permute-done.1.outer, s32[1]{0:T(128)} %constant.56.clone.1._), custom_call_target="tpu_custom_call" | custom-call | flops 268435456 | bytes 8388608 | tf_op jit(solution)/shard_map/pallas_call | solution.py:360
  33.1 2.2 %shard_map.85.shifts = bf16[4,10,128,768]{3,2,1,0:T(8,128)(2,1)S(1)} custom-call(s32[4]{0:T(128)S(1)} %get-tuple-element.38.at, bf16[4,8,128,256]{3,2,1,0:T(8,128)(2,1)S(1)} %bitcast.37, bf16[4,1,128,256]{3,2,1,0:T(8,128)(2,1)S(1)} %collective-permute-done.inner, ...), custom_call_target="tpu_custom_call", output_to_operand_aliasing={{}: (4, {})} | custom-call | flops 268435456 | bytes 8388608 | tf_op jit(solution)/shard_map/pallas_call | solution.py:360
  35.6 3.4 %collective-permute-start.6 = (bf16[384,256]{1,0:T(8,128)(2,1)S(1)}, bf16[384,256]{1,0:T(8,128)(2,1)S(1)}, u32[]{:S(2)}, u32[]{:S(2)}) collective-permute-start(bf16[384,256]{1,0:T(8,128)(2,1)S(1)} %dynamic-slice_bitcast_fusion.3), channel_id=1, source_target_pairs={{0,2},{1,7},{2,4},{3,1},{4,6},{5,3},{6,0},{7,5},{8,10},{9,15},{10,... | collective-permute-start | bytes 589832 | tf_op jit(solution)/shard_map/ppermute | solution.py:45
  39.1 2.6 %collective-permute-done.6 = bf16[384,256]{1,0:T(8,128)(2,1)S(1)} collective-permute-done((bf16[384,256]{1,0:T(8,128)(2,1)S(1)}, bf16[384,256]{1,0:T(8,128)(2,1)S(1)}, u32[]{:S(2)}, u32[]{:S(2)}) %collective-permute-start.6) | collective-permute-done | bytes 196640 | tf_op jit(solution)/shard_map/ppermute | solution.py:45
  41.7 1.8 %collective-permute-start.7 = (bf16[384,256]{1,0:T(8,128)(2,1)S(1)}, bf16[384,256]{1,0:T(8,128)(2,1)S(1)}, u32[]{:S(2)}, u32[]{:S(2)}) collective-permute-start(bf16[384,256]{1,0:T(8,128)(2,1)S(1)} %collective-permute-done.6), channel_id=1, source_target_pairs={{0,1},{1,0},{2,3},{3,2},{4,5},{5,4},{6,7},{7,6},{8,9},{9,8},{10,11... | collective-permute-start | bytes 589832 | tf_op jit(solution)/shard_map/ppermute | solution.py:45
  45.2 5.2 %shard_map.87 = (bf16[4,8,128,256]{3,2,1,0:T(8,128)(2,1)S(1)}, bf16[4,8,128,256]{3,2,1,0:T(8,128)(2,1)S(1)}, bf16[4,1,128,256]{3,2,1,0:T(8,128)(2,1)}, bf16[4,1,128,256]{3,2,1,0:T(8,128)(2,1)}) custom-call(s32[4]{0:T(128)S(1)} %get-tuple-element.39.at, bf16[4,10,128,768]{3,2,1,0:T(8,128)(2,1)S(1)} %shard_map.85.shifts, ...), custom_call_target="tpu_custom_call" | custom-call | flops 6442450944 | bytes 8388608 | tf_op jit(solution)/shard_map/pallas_call | solution.py:435
  50.4 3.4 %collective-permute-done.2.ahead1.ahead2 = bf16[2,8,128,256]{3,2,1,0:T(8,128)(2,1)} collective-permute-done((bf16[2,8,128,256]{3,2,1,0:T(8,128)(2,1)}, bf16[2,8,128,256]{3,2,1,0:T(8,128)(2,1)}, u32[]{:S(2)}, u32[]{:S(2)}) %collective-permute-start.2) | collective-permute-done | bytes 1048608 | tf_op jit(solution)/shard_map/ppermute | solution.py:128
  53.8 6.5 %shard_map.88 = (bf16[4,8,128,256]{3,2,1,0:T(8,128)(2,1)S(1)}, bf16[4,8,128,256]{3,2,1,0:T(8,128)(2,1)S(1)}, bf16[4,1,128,256]{3,2,1,0:T(8,128)(2,1)}, bf16[4,1,128,256]{3,2,1,0:T(8,128)(2,1)}) custom-call(s32[4]{0:T(128)S(1)} %get-tuple-element.38.at, ...), custom_call_target="tpu_custom_call", output_to_operand_aliasing={{0}: (9, {}), {1}: (10, {}), {2}: (11, {}), {3}: (12, {})} | custom-call | flops 6442450944 | bytes 8388608 | tf_op jit(solution)/shard_map/pallas_call | solution.py:435
  60.3 10.3 %shard_map.92 = (f32[2,384,256]{2,1,0:T(8,128)S(1)}, f32[384,256]{1,0:T(8,128)S(1)}, f32[384,256]{1,0:T(8,128)S(1)}, f32[2,384,256]{2,1,0:T(8,128)S(1)}, f32[2,384,256]{2,1,0:T(8,128)S(1)}) custom-call(s32[4]{0:T(128)S(1)} %get-tuple-element.39.at, bf16[4,10,128,768]{3,2,1,0:T(8,128)(2,1)S(1)} %shard_map.85.shifts, ...), custom_call_target="tpu_custom_call" | custom-call | flops 6442450944 | bytes 8388608 | tf_op jit(solution)/shard_map/pallas_call | solution.py:453
  72.5 1.7 %collective-permute-start.13 = (f32[384,256]{1,0:T(8,128)S(1)}, f32[384,256]{1,0:T(8,128)S(1)}, u32[]{:S(2)}, u32[]{:S(2)}) collective-permute-start(f32[384,256]{1,0:T(8,128)S(1)} %add.80), channel_id=1, source_target_pairs={{0,2},{1,7},{2,4},{3,1},{4,6},{5,3},{6,0},{7,5},{8,10},{9,15},{10,... | collective-permute-start | bytes 1179656 | tf_op jit(solution)/shard_map/ppermute | solution.py:45
  74.1 5.5 %collective-permute-done.13 = f32[384,256]{1,0:T(8,128)S(1)} collective-permute-done((f32[384,256]{1,0:T(8,128)S(1)}, f32[384,256]{1,0:T(8,128)S(1)}, u32[]{:S(2)}, u32[]{:S(2)}) %collective-permute-start.13) | collective-permute-done | bytes 393248 | tf_op jit(solution)/shard_map/ppermute | solution.py:45
  79.9 2.4 %collective-permute-start.14 = (bf16[2,384,256]{2,1,0:T(8,128)(2,1)S(1)}, bf16[2,384,256]{2,1,0:T(8,128)(2,1)S(1)}, u32[]{:S(2)}, u32[]{:S(2)}) collective-permute-start(bf16[2,384,256]{2,1,0:T(8,128)(2,1)S(1)} %add_convert_fusion), channel_id=1, source_target_pairs={{0,2},{1,7},{2,4},{3,1},{4,6},{5,3},{6,0},{7,5},{8,10},{9,15},{10,... | collective-permute-start | bytes 1179656 | tf_op jit(solution)/shard_map/ppermute | solution.py:45
  82.3 4.7 %collective-permute-done.14 = bf16[2,384,256]{2,1,0:T(8,128)(2,1)S(1)} collective-permute-done((bf16[2,384,256]{2,1,0:T(8,128)(2,1)S(1)}, bf16[2,384,256]{2,1,0:T(8,128)(2,1)S(1)}, u32[]{:S(2)}, u32[]{:S(2)}) %collective-permute-start.14) | collective-permute-done | bytes 393248 | tf_op jit(solution)/shard_map/ppermute | solution.py:45
  87.1 4.2 %collective-permute-start.15 = (f32[16,24,256]{2,1,0:T(8,128)S(1)}, f32[16,24,256]{2,1,0:T(8,128)S(1)}, u32[]{:S(2)}, u32[]{:S(2)}) collective-permute-start(f32[16,24,256]{2,1,0:T(8,128)S(1)} %dynamic-slice_bitcast_fusion), channel_id=1, source_target_pairs={{0,1},{1,0},{2,3},{3,2},{4,5},{5,4},{6,7},{7,6},{8,9},{9,8},{10,11... | collective-permute-start | bytes 1179656 | tf_op jit(solution)/shard_map/ppermute | solution.py:45
  92.4 1.9 %collective-permute-start.8 = (bf16[2,8,128,256]{3,2,1,0:T(8,128)(2,1)}, bf16[2,8,128,256]{3,2,1,0:T(8,128)(2,1)S(1)}, u32[]{:S(2)}, u32[]{:S(2)}) collective-permute-start(bf16[2,8,128,256]{3,2,1,0:T(8,128)(2,1)} %slice.17), channel_id=1, source_target_pairs={{0,16},{16,32},{32,48},{48,64},{64,80},{80,96},{96,112},{1,17},{17... | collective-permute-start | bytes 3145736 | tf_op jit(solution)/shard_map/ppermute | solution.py:128
  94.3 1.9 %collective-permute-start.10 = (bf16[4,1,128,256]{3,2,1,0:T(8,128)(2,1)}, bf16[4,1,128,256]{3,2,1,0:T(8,128)(2,1)}, u32[]{:S(2)}, u32[]{:S(2)}) collective-permute-start(bf16[4,1,128,256]{3,2,1,0:T(8,128)(2,1)} %get-tuple-element.30), channel_id=1, source_target_pairs={{1,2},{2,1},{3,4},{4,3},{5,6},{6,5},{7,8},{8,7},{9,10},{10,9},{11,... | collective-permute-start | bytes 786440 | tf_op jit(solution)/shard_map/ppermute | solution.py:114
  98.6 9.1 %all-to-all-start.1 = ((f32[16,24,256]{2,1,0:T(8,128)}), f32[16,24,256]{2,1,0:T(8,128)}, u32[]{:S(2)}, u32[]{:S(2)}) async-start(f32[16,24,256]{2,1,0:T(8,128)} %bitcast_add_fusion), calls=%async_computation.1 | async-start | bytes 786432 | tf_op jit(solution)/shard_map/all_to_all | solution.py:105
  107.7 1.6 %copy-done.1 = bf16[1,4,8,128,256]{4,3,2,1,0:T(8,128)(2,1)S(1)} copy-done((bf16[1,4,8,128,256]{4,3,2,1,0:T(8,128)(2,1)S(1)}, bf16[1,4,8,128,256]{4,3,2,1,0:T(8,128)(2,1)}, u32[]{:S(2)}) %copy-start.1) | copy-done | bytes 2097176
  109.3 1.3 copy-done.3
  110.6 1.6 %copy-done.5 = bf16[1,4,8,128,256]{4,3,2,1,0:T(8,128)(2,1)S(1)} copy-done((bf16[1,4,8,128,256]{4,3,2,1,0:T(8,128)(2,1)S(1)}, bf16[1,4,8,128,256]{4,3,2,1,0:T(8,128)(2,1)}, u32[]{:S(2)}) %copy-start.5) | copy-done | bytes 2097176
  112.2 1.6 %copy-done.8 = bf16[4,8,128,256]{3,2,1,0:T(8,128)(2,1)S(1)} copy-done((bf16[4,8,128,256]{3,2,1,0:T(8,128)(2,1)S(1)}, bf16[4,8,128,256]{3,2,1,0:T(8,128)(2,1)}, u32[]{:S(2)}) %copy-start.8) | copy-done | bytes 2097176
  113.7 9.6 %shard_map.91 = bf16[4,8,128,256]{3,2,1,0:T(8,128)(2,1)} custom-call(s32[4]{0:T(128)S(1)} %get-tuple-element.39.at, bf16[4,8,128,256]{3,2,1,0:T(8,128)(2,1)S(1)} %copy-done.8, bf16[4,1,128,256]{3,2,1,0:T(8,128)(2,1)} %collective-permute-done.9.inner, bf16[4,1,128,256]{3,2,1,0:T(8,128)(2,1)} %collective-permute-done.10.outer, ...), custom_call_target="tpu_custom_call" | custom-call | flops 4831838208 | bytes 8388608 | tf_op jit(solution)/shard_map/pallas_call | solution.py:360
  123.3 6.5 %collective-permute-done.8.past0.past1 = bf16[2,8,128,256]{3,2,1,0:T(8,128)(2,1)S(1)} collective-permute-done((bf16[2,8,128,256]{3,2,1,0:T(8,128)(2,1)}, bf16[2,8,128,256]{3,2,1,0:T(8,128)(2,1)S(1)}, u32[]{:S(2)}, u32[]{:S(2)}) %collective-permute-start.8) | collective-permute-done | bytes 1048608 | tf_op jit(solution)/shard_map/ppermute | solution.py:128
  129.8 3.9 %shard_map.89 = bf16[4,8,128,256]{3,2,1,0:T(8,128)(2,1)} custom-call(s32[4]{0:T(128)S(1)} %get-tuple-element.39.at, bf16[4,8,128,256]{3,2,1,0:T(8,128)(2,1)S(1)} %bitcast.39, bf16[2,8,128,256]{3,2,1,0:T(8,128)(2,1)S(1)} %collective-permute-done.8.past0.past1, bf16[2,8,128,256]{3,2,1,0:T(8,128)(2,1)S(1)} %collective-permute-done.8.past0.past1, ...), custom_call_target="tpu_custom_call" | custom-call | flops 1610612736 | bytes 8388608 | tf_op jit(solution)/shard_map/pallas_call | solution.py:360
  (56 shorter events, 11.9 us)
Async XLA Ops:
  2.1 13.3 %all-to-all-start = ((bf16[16,24,256]{2,1,0:T(8,128)(2,1)}), bf16[16,24,256]{2,1,0:T(8,128)(2,1)S(1)}, u32[]{:S(2)}, u32[]{:S(2)}) async-start(bf16[16,24,256]{2,1,0:T(8,128)(2,1)} %broadcast_in_dim.41), calls=%async_computation | async-start | bytes 393216 | tf_op jit(solution)/shard_map/all_to_all | solution.py:85
  15.3 7.3 %collective-permute-start.3 = (bf16[384,256]{1,0:T(8,128)(2,1)S(1)}, bf16[384,256]{1,0:T(8,128)(2,1)S(1)}, u32[]{:S(2)}, u32[]{:S(2)}) collective-permute-start(bf16[384,256]{1,0:T(8,128)(2,1)S(1)} %bitcast.56), channel_id=1, source_target_pairs={{0,1},{1,0},{2,3},{3,2},{4,5},{5,4},{6,7},{7,6},{8,9},{9,8},{10,11... | collective-permute-start | bytes 589832 | tf_op jit(solution)/shard_map/ppermute | solution.py:45
  19.0 11.9 %collective-permute-start = (bf16[4,1,128,256]{3,2,1,0:T(8,128)(2,1)}, bf16[4,1,128,256]{3,2,1,0:T(8,128)(2,1)S(1)}, u32[]{:S(2)}, u32[]{:S(2)}) collective-permute-start(bf16[4,1,128,256]{3,2,1,0:T(8,128)(2,1)} %get-tuple-element.37), channel_id=1, source_target_pairs={{0,1},{1,0},{2,3},{3,2},{4,5},{5,4},{6,7},{7,6},{8,9},{9,8},{10,11... | collective-permute-start | bytes 786440 | tf_op jit(solution)/shard_map/ppermute | solution.py:45
  19.0 11.9 %collective-permute-start.1 = (bf16[4,1,128,256]{3,2,1,0:T(8,128)(2,1)}, bf16[4,1,128,256]{3,2,1,0:T(8,128)(2,1)S(1)}, u32[]{:S(2)}, u32[]{:S(2)}) collective-permute-start(bf16[4,1,128,256]{3,2,1,0:T(8,128)(2,1)} %get-tuple-element.36), channel_id=1, source_target_pairs={{1,2},{2,1},{3,4},{4,3},{5,6},{6,5},{7,8},{8,7},{9,10},{10,9},{11,... | collective-permute-start | bytes 786440 | tf_op jit(solution)/shard_map/ppermute | solution.py:114
  22.5 8.4 %copy-start = (bf16[1,4,8,128,256]{4,3,2,1,0:T(8,128)(2,1)S(1)}, bf16[1,4,8,128,256]{4,3,2,1,0:T(8,128)(2,1)}, u32[]{:S(2)}) copy-start(bf16[1,4,8,128,256]{4,3,2,1,0:T(8,128)(2,1)} %param.5) | copy-start | bytes 6291460
  22.6 12.7 %collective-permute-start.4 = (bf16[2,384,256]{2,1,0:T(8,128)(2,1)S(1)}, bf16[2,384,256]{2,1,0:T(8,128)(2,1)S(1)}, u32[]{:S(2)}, u32[]{:S(2)}) collective-permute-start(bf16[2,384,256]{2,1,0:T(8,128)(2,1)S(1)} %bitcast_dynamic-update-slice_fusion.5), channel_id=1, source_target_pairs={{0,2},{1,7},{2,4},{3,1},{4,6},{5,3},{6,0},{7,5},{8,10},{9,15},{10,... | collective-permute-start | bytes 1179656 | tf_op jit(solution)/shard_map/ppermute | solution.py:45
  27.3 26.5 %collective-permute-start.2 = (bf16[2,8,128,256]{3,2,1,0:T(8,128)(2,1)}, bf16[2,8,128,256]{3,2,1,0:T(8,128)(2,1)}, u32[]{:S(2)}, u32[]{:S(2)}) collective-permute-start(bf16[2,8,128,256]{3,2,1,0:T(8,128)(2,1)} %slice_bitcast_fusion), channel_id=1, source_target_pairs={{16,0},{32,16},{48,32},{64,48},{80,64},{96,80},{112,96},{17,1},{33... | collective-permute-start | bytes 3145736 | tf_op jit(solution)/shard_map/ppermute | solution.py:128
  35.3 8.2 %collective-permute-start.5 = (bf16[2,384,256]{2,1,0:T(8,128)(2,1)S(1)}, bf16[2,384,256]{2,1,0:T(8,128)(2,1)S(1)}, u32[]{:S(2)}, u32[]{:S(2)}) collective-permute-start(bf16[2,384,256]{2,1,0:T(8,128)(2,1)S(1)} %collective-permute-done.4), channel_id=1, source_target_pairs={{0,1},{1,0},{2,3},{3,2},{4,5},{5,4},{6,7},{7,6},{8,9},{9,8},{10,11... | collective-permute-start | bytes 1179656 | tf_op jit(solution)/shard_map/ppermute | solution.py:45
  35.6 9.0 %copy-start.6 = (bf16[192,192]{1,0:T(8,128)(2,1)S(1)}, bf16[192,192]{1,0:T(8,128)(2,1)}, u32[]{:S(2)}) copy-start(bf16[192,192]{1,0:T(8,128)(2,1)} %constant.69.clone.order) | copy-start | bytes 221188
  35.6 6.1 %collective-permute-start.6 = (bf16[384,256]{1,0:T(8,128)(2,1)S(1)}, bf16[384,256]{1,0:T(8,128)(2,1)S(1)}, u32[]{:S(2)}, u32[]{:S(2)}) collective-permute-start(bf16[384,256]{1,0:T(8,128)(2,1)S(1)} %dynamic-slice_bitcast_fusion.3), channel_id=1, source_target_pairs={{0,2},{1,7},{2,4},{3,1},{4,6},{5,3},{6,0},{7,5},{8,10},{9,15},{10,... | collective-permute-start | bytes 589832 | tf_op jit(solution)/shard_map/ppermute | solution.py:45
  39.1 6.2 %copy-start.4 = (bf16[1,4,8,128,256]{4,3,2,1,0:T(8,128)(2,1)S(1)}, bf16[1,4,8,128,256]{4,3,2,1,0:T(8,128)(2,1)}, u32[]{:S(2)}) copy-start(bf16[1,4,8,128,256]{4,3,2,1,0:T(8,128)(2,1)} %param.8) | copy-start | bytes 6291460
  41.7 2.9 %collective-permute-start.7 = (bf16[384,256]{1,0:T(8,128)(2,1)S(1)}, bf16[384,256]{1,0:T(8,128)(2,1)S(1)}, u32[]{:S(2)}, u32[]{:S(2)}) collective-permute-start(bf16[384,256]{1,0:T(8,128)(2,1)S(1)} %collective-permute-done.6), channel_id=1, source_target_pairs={{0,1},{1,0},{2,3},{3,2},{4,5},{5,4},{6,7},{7,6},{8,9},{9,8},{10,11... | collective-permute-start | bytes 589832 | tf_op jit(solution)/shard_map/ppermute | solution.py:45
  60.3 10.3 %copy-start.7 = (bf16[4,8,128,256]{3,2,1,0:T(8,128)(2,1)}, bf16[4,8,128,256]{3,2,1,0:T(8,128)(2,1)S(1)}, u32[]{:S(2)}) copy-start(bf16[4,8,128,256]{3,2,1,0:T(8,128)(2,1)S(1)} %get-tuple-element.28.grad_pre) | copy-start | bytes 6291460
  70.6 1.8 %collective-permute-start.12 = (f32[384,256]{1,0:T(8,128)S(1)}, f32[384,256]{1,0:T(8,128)S(1)}, u32[]{:S(2)}, u32[]{:S(2)}) collective-permute-start(f32[384,256]{1,0:T(8,128)S(1)} %get-tuple-element.35), channel_id=1, source_target_pairs={{0,1},{1,0},{2,3},{3,2},{4,5},{5,4},{6,7},{7,6},{8,9},{9,8},{10,11... | collective-permute-start | bytes 1179656 | tf_op jit(solution)/shard_map/ppermute | solution.py:45
  70.9 8.8 %collective-permute-start.11 = (f32[2,384,256]{2,1,0:T(8,128)S(1)}, f32[2,384,256]{2,1,0:T(8,128)S(1)}, u32[]{:S(2)}, u32[]{:S(2)}) collective-permute-start(f32[2,384,256]{2,1,0:T(8,128)S(1)} %get-tuple-element.33), channel_id=1, source_target_pairs={{0,1},{1,0},{2,3},{3,2},{4,5},{5,4},{6,7},{7,6},{8,9},{9,8},{10,11... | collective-permute-start | bytes 2359304 | tf_op jit(solution)/shard_map/ppermute | solution.py:45
  72.5 7.2 %collective-permute-start.13 = (f32[384,256]{1,0:T(8,128)S(1)}, f32[384,256]{1,0:T(8,128)S(1)}, u32[]{:S(2)}, u32[]{:S(2)}) collective-permute-start(f32[384,256]{1,0:T(8,128)S(1)} %add.80), channel_id=1, source_target_pairs={{0,2},{1,7},{2,4},{3,1},{4,6},{5,3},{6,0},{7,5},{8,10},{9,15},{10,... | collective-permute-start | bytes 1179656 | tf_op jit(solution)/shard_map/ppermute | solution.py:45
  79.9 7.1 %collective-permute-start.14 = (bf16[2,384,256]{2,1,0:T(8,128)(2,1)S(1)}, bf16[2,384,256]{2,1,0:T(8,128)(2,1)S(1)}, u32[]{:S(2)}, u32[]{:S(2)}) collective-permute-start(bf16[2,384,256]{2,1,0:T(8,128)(2,1)S(1)} %add_convert_fusion), channel_id=1, source_target_pairs={{0,2},{1,7},{2,4},{3,1},{4,6},{5,3},{6,0},{7,5},{8,10},{9,15},{10,... | collective-permute-start | bytes 1179656 | tf_op jit(solution)/shard_map/ppermute | solution.py:45
  87.1 10.6 %collective-permute-start.15 = (f32[16,24,256]{2,1,0:T(8,128)S(1)}, f32[16,24,256]{2,1,0:T(8,128)S(1)}, u32[]{:S(2)}, u32[]{:S(2)}) collective-permute-start(f32[16,24,256]{2,1,0:T(8,128)S(1)} %dynamic-slice_bitcast_fusion), channel_id=1, source_target_pairs={{0,1},{1,0},{2,3},{3,2},{4,5},{5,4},{6,7},{7,6},{8,9},{9,8},{10,11... | collective-permute-start | bytes 1179656 | tf_op jit(solution)/shard_map/ppermute | solution.py:45
  92.4 37.4 %collective-permute-start.8 = (bf16[2,8,128,256]{3,2,1,0:T(8,128)(2,1)}, bf16[2,8,128,256]{3,2,1,0:T(8,128)(2,1)S(1)}, u32[]{:S(2)}, u32[]{:S(2)}) collective-permute-start(bf16[2,8,128,256]{3,2,1,0:T(8,128)(2,1)} %slice.17), channel_id=1, source_target_pairs={{0,16},{16,32},{32,48},{48,64},{64,80},{80,96},{96,112},{1,17},{17... | collective-permute-start | bytes 3145736 | tf_op jit(solution)/shard_map/ppermute | solution.py:128
  94.3 13.4 %collective-permute-start.10 = (bf16[4,1,128,256]{3,2,1,0:T(8,128)(2,1)}, bf16[4,1,128,256]{3,2,1,0:T(8,128)(2,1)}, u32[]{:S(2)}, u32[]{:S(2)}) collective-permute-start(bf16[4,1,128,256]{3,2,1,0:T(8,128)(2,1)} %get-tuple-element.30), channel_id=1, source_target_pairs={{1,2},{2,1},{3,4},{4,3},{5,6},{6,5},{7,8},{8,7},{9,10},{10,9},{11,... | collective-permute-start | bytes 786440 | tf_op jit(solution)/shard_map/ppermute | solution.py:114
  96.3 11.4 %collective-permute-start.9 = (bf16[4,1,128,256]{3,2,1,0:T(8,128)(2,1)}, bf16[4,1,128,256]{3,2,1,0:T(8,128)(2,1)}, u32[]{:S(2)}, u32[]{:S(2)}) collective-permute-start(bf16[4,1,128,256]{3,2,1,0:T(8,128)(2,1)} %get-tuple-element.29), channel_id=1, source_target_pairs={{0,1},{1,0},{2,3},{3,2},{4,5},{5,4},{6,7},{7,6},{8,9},{9,8},{10,11... | collective-permute-start | bytes 786440 | tf_op jit(solution)/shard_map/ppermute | solution.py:45
  96.7 1.0 copy-start.2
  98.6 35.5 %all-to-all-start.1 = ((f32[16,24,256]{2,1,0:T(8,128)}), f32[16,24,256]{2,1,0:T(8,128)}, u32[]{:S(2)}, u32[]{:S(2)}) async-start(f32[16,24,256]{2,1,0:T(8,128)} %bitcast_add_fusion), calls=%async_computation.1 | async-start | bytes 786432 | tf_op jit(solution)/shard_map/all_to_all | solution.py:105
  107.7 1.6 %copy-start.1 = (bf16[1,4,8,128,256]{4,3,2,1,0:T(8,128)(2,1)S(1)}, bf16[1,4,8,128,256]{4,3,2,1,0:T(8,128)(2,1)}, u32[]{:S(2)}) copy-start(bf16[1,4,8,128,256]{4,3,2,1,0:T(8,128)(2,1)} %param.5) | copy-start | bytes 6291460
  109.3 1.3 copy-start.3
  110.6 1.6 %copy-start.5 = (bf16[1,4,8,128,256]{4,3,2,1,0:T(8,128)(2,1)S(1)}, bf16[1,4,8,128,256]{4,3,2,1,0:T(8,128)(2,1)}, u32[]{:S(2)}) copy-start(bf16[1,4,8,128,256]{4,3,2,1,0:T(8,128)(2,1)} %param.8) | copy-start | bytes 6291460
  112.2 1.6 %copy-start.8 = (bf16[4,8,128,256]{3,2,1,0:T(8,128)(2,1)S(1)}, bf16[4,8,128,256]{3,2,1,0:T(8,128)(2,1)}, u32[]{:S(2)}) copy-start(bf16[4,8,128,256]{3,2,1,0:T(8,128)(2,1)} %copy-done.7) | copy-start | bytes 6291460
